TPU v7x, 32 devices: a whole 2x2x4 slice. The times are simulated.
32 devices in a mesh: dp: 8 (over y, x, core), space: 4 (over z).
Axes of the slice: x: 2, y: 2, z: 4, core: 2. Of those that a mesh axis runs over, the one named last changes fastest.
Arguments:
- features: bfloat16 [8, 32, 16, 512], P('dp', 'space'), may hold values from -48 to 48
- cotangent: bfloat16 [8, 32, 16, 512], P('dp', 'space'), may hold values from -6 to 6
- dw_kernel: float32 [7, 7, 512], replicated, may hold values from -0.875 to 0.875
- ln_gain: float32 [512], replicated, may hold values from 0.1 to 1.9
- ln_bias: float32 [512], replicated, may hold values from -3 to 3
- layer_scale: float32 [512], replicated, may hold values from 0.3 to 3
- w_up: bfloat16 [512, 2048], P('dp'), may hold values from -0.25 to 0.25
- w_down: bfloat16 [2048, 512], P('dp'), may hold values from -0.125 to 0.125
Outputs:
- result: bfloat16 [8, 32, 16, 512], P('dp', 'space')
- d_features: float32 [8, 32, 16, 512], P('dp', 'space')
- d_w_up: float32 [512, 2048], P('dp', 'space')
- d_w_down: float32 [2048, 512], P('space', 'dp')
- d_kernel: float32 [7, 7, 512], replicated
- d_gain: float32 [512], replicated
- d_bias: float32 [512], replicated
- d_scale: float32 [512], replicated
All inputs are finite; a program needn't handle non-finite values.
Results may differ from a plain program's by a relative error of at most 0.0065.
Values may be sent and summed in bfloat16 or wider, within the bound.
A program may use at most 64 MiB of HBM per device.

v0:
```python
import math

import jax
import jax.numpy as jnp
from jax import lax
from jax.sharding import PartitionSpec as P

D = 512
KW = 7


def extended_2(cells, sides, width):
    for axis, dim in sides:
        count = lax.axis_size(axis)
        ends = count - 1
        head = lax.slice_in_dim(cells, 0, width, axis=dim)
        tail = lax.slice_in_dim(cells, cells.shape[dim] - width, cells.shape[dim], axis=dim)
        cells = jnp.concatenate(
            [
                lax.ppermute(tail, axis, [(i, (i + 1) % count) for i in range(ends)]),
                cells,
                lax.ppermute(head, axis, [((i + 1) % count, i) for i in range(ends)]),
            ],
            axis=dim,
        )
    return cells


def gelu_pair(preact):
    cumulative = 0.5 * (1.0 + jax.scipy.special.erf(preact * (1.0 / math.sqrt(2.0))))
    density = jnp.exp(-0.5 * preact * preact) * (1.0 / math.sqrt(2.0 * math.pi))
    return (preact * cumulative, cumulative + preact * density)


def depthwise(padded, kernel, num_rows, num_cols):
    summed = jnp.zeros((num_rows, num_cols, padded.shape[-1]), jnp.float32)
    for row_off in range(kernel.shape[0]):
        for col_off in range(kernel.shape[1]):
            summed = (
                summed
                + kernel[row_off, col_off]
                * padded[row_off : row_off + num_rows, col_off : col_off + num_cols]
            )
    return summed


def kernel_grad(padded, upstream):
    num_rows, num_cols = (upstream.shape[0], upstream.shape[1])
    entries = []
    for row_off in range(KW):
        for col_off in range(KW):
            window = padded[row_off : row_off + num_rows, col_off : col_off + num_cols]
            entries.append(jnp.sum(window * upstream, axis=(0, 1)))
    return jnp.stack(entries).reshape(KW, KW, upstream.shape[-1])


def with_rim(source, margin):
    extended = extended_2(source, (("space", 0),), margin)
    return jnp.pad(extended.astype(jnp.float32), ((0, 0), (margin, margin), (0, 0)))


def local(features, cotangent, dw_kernel, ln_gain, ln_bias, layer_scale, w_up, w_down):
    margin = KW // 2
    up_full, down_full = (
        lax.all_gather(w_up, "dp", axis=0, tiled=True),
        lax.all_gather(w_down, "dp", axis=0, tiled=True),
    )
    local_x = features[0]
    num_rows, num_cols = (local_x.shape[0], local_x.shape[1])
    padded = with_rim(local_x, margin)
    conv_out = depthwise(padded, dw_kernel, num_rows, num_cols)
    center = conv_out - jnp.mean(conv_out, axis=-1, keepdims=True)
    inverse = lax.rsqrt(jnp.mean(center * center, axis=-1, keepdims=True) + 1e-06)
    scaled = center * inverse
    tokens = (scaled * ln_gain + ln_bias).astype(jnp.bfloat16).reshape(-1, D)
    scaled_rows = scaled.reshape(-1, D)
    preact = jnp.dot(tokens, up_full, preferred_element_type=jnp.float32)
    activation, slope = gelu_pair(preact)
    hidden_act = activation.astype(jnp.bfloat16)
    mixed = jnp.dot(hidden_act, down_full, preferred_element_type=jnp.float32)
    result = (local_x.astype(jnp.float32).reshape(-1, D) + layer_scale * mixed).astype(jnp.bfloat16)
    cot_rows = cotangent[0].reshape(-1, D).astype(jnp.float32)
    d_mixed = (layer_scale * cot_rows).astype(jnp.bfloat16)
    d_hidden = jnp.dot(d_mixed, down_full.T, preferred_element_type=jnp.float32)
    d_pre = (d_hidden * slope).astype(jnp.bfloat16)
    d_norm = jnp.dot(d_pre, up_full.T, preferred_element_type=jnp.float32)
    d_hat = d_norm * ln_gain
    first = jnp.mean(d_hat, axis=-1, keepdims=True)
    second = jnp.mean(d_hat * scaled_rows, axis=-1, keepdims=True)
    d_conv = (inverse.reshape(-1, 1) * (d_hat - first - scaled_rows * second)).astype(jnp.bfloat16)
    d_conv_grid = d_conv.reshape(num_rows, num_cols, D)
    pad_grad = with_rim(d_conv_grid, margin)
    d_feat = cot_rows.reshape(num_rows, num_cols, D) + depthwise(
        pad_grad, dw_kernel[::-1, ::-1], num_rows, num_cols
    )
    d_grid = d_conv_grid.astype(jnp.float32)
    region_in, region_grad = (
        lax.all_gather(tokens, "space", axis=0, tiled=True),
        lax.all_gather(d_mixed, "space", axis=0, tiled=True),
    )
    hidden_cols, d_pre_cols = (
        lax.all_to_all(hidden_act, "space", split_axis=1, concat_axis=0, tiled=True),
        lax.all_to_all(d_pre, "space", split_axis=1, concat_axis=0, tiled=True),
    )
    up_part = jnp.dot(region_in.T, d_pre_cols, preferred_element_type=jnp.float32)
    down_part = jnp.dot(hidden_cols.T, region_grad, preferred_element_type=jnp.float32)
    grad_up, grad_down = (
        lax.psum_scatter(up_part, "dp", scatter_dimension=0, tiled=True),
        lax.psum_scatter(down_part, "dp", scatter_dimension=1, tiled=True),
    )
    grad_kernel, grad_gain, grad_bias, grad_scale = lax.psum(
        (
            kernel_grad(padded, d_grid),
            jnp.sum(d_norm * scaled_rows, axis=0),
            jnp.sum(d_norm, axis=0),
            jnp.sum(cot_rows * mixed, axis=0),
        ),
        ("dp", "space"),
    )
    regions = float(lax.axis_size("dp"))
    return (
        result.reshape(1, num_rows, num_cols, D),
        d_feat.reshape(1, num_rows, num_cols, D),
        grad_up / regions,
        grad_down / regions,
        grad_kernel / regions,
        grad_gain / regions,
        grad_bias / regions,
        grad_scale / regions,
    )


def solution(mesh):
    in_specs = (
        P("dp", "space", None, None),
        P("dp", "space", None, None),
        P(),
        P(),
        P(),
        P(),
        P("dp", None),
        P("dp", None),
    )
    out_specs = (
        P("dp", "space", None, None),
        P("dp", "space", None, None),
        P("dp", "space"),
        P("space", "dp"),
        P(),
        P(),
        P(),
        P(),
    )
    return jax.shard_map(local, mesh=mesh, in_specs=in_specs, out_specs=out_specs, check_vma=False)
```

profile of v0, /device:TPU:0, one launch (start us, length us, event | category | flops | bytes accessed | tf_op | source)
XLA Modules:
  0.0 300.9 jit_solution(16542983574361493612)
XLA Ops:
  7.2 0.7 all-gather.3.cloned.1.call-update
  7.9 0.7 all-gather.5.cloned.1.call-update
  8.7 0.8 slice_bitcast_fusion.1
  9.5 1.3 collective-permute-start.1
  10.8 5.6 %collective-permute-start = (bf16[3,16,512]{2,1,0:T(8,128)(2,1)S(1)}, bf16[3,16,512]{2,1,0:T(8,128)(2,1)S(1)}, u32[]{:S(2)}, u32[]{:S(2)}) collective-permute-start(bf16[3,16,512]{2,1,0:T(8,128)(2,1)S(1)} %get-tuple-element.74), channel_id=1, source_target_pairs={{0,1},{1,2},{2,3},{4,5},{5,6},{6,7},{8,9},{9,10},{10,11},{12,13},{... | collective-permute-start | bytes 147464 | tf_op jit(solution)/shard_map/ppermute | solution.py:20
  16.4 1.1 fusion.157
  17.5 1.2 fusion.158
  18.9 0.9 fusion.159
  20.0 0.9 maximum_convert_fusion
  20.9 2.0 fusion.155
  22.9 0.2 multiply_reduce_fusion
  23.1 0.6 rsqrt.16
  23.7 0.1 add_convert_fusion
  24.1 17.3 %all_gather.14 = bf16[512,512]{1,0:T(8,128)(2,1)} all-gather(bf16[128,512]{1,0:T(8,128)(2,1)S(1)} %bitcast.219), channel_id=1, replica_groups=mesh['dp'=8,'space'=4] {'space'}, dimensions={0}, use_global_device_ids=true | all-gather | bytes 655360 | tf_op jit(solution)/shard_map/all_gather | solution.py:98
  41.4 2.1 multiply_convert_fusion
  43.6 26.5 %all-gather.5.cloned.1.call-done = bf16[2048,512]{1,0:T(8,128)(2,1)} async-done(((bf16[256,512]{1,0:T(8,128)(2,1)}), bf16[2048,512]{1,0:T(8,128)(2,1)}) %all-gather.5.cloned.1.call-update) | async-done | bytes 2097168 | tf_op jit(solution)/shard_map/all_gather | solution.py:66
  70.1 3.4 %fusion.153 = (f32[512]{0:T(512)}, bf16[128,512]{1,0:T(8,128)(2,1)}, bf16[128,512]{1,0:T(8,128)(2,1)S(1)}) fusion(bf16[1,8,16,512]{3,2,1,0:T(8,128)(2,1)S(1)} %copy-done.5, f32[512]{0:T(512)S(1)} %copy-done.74, bf16[1,8,16,512]{3,2,1,0:T(8,128)(2,1)S(1)} %copy-done.4, bf16[128,2048]{1,0:T(8,128)(2,1)S(1)} %get-tuple-element.125, ...), kind=kOutput, calls=%fused_computation.306 | convolution fusion | flops 269024768 | bytes 3149824 | tf_op jit(solution)/shard_map/dot_general | solution.py:80
  73.6 0.7 copy-done.7
  74.2 0.9 fusion
  75.1 0.8 copy-done.1
  75.9 0.9 copy.23
  76.7 4.6 %all-to-all-start = ((bf16[128,4,512]{2,0,1:T(8,128)(2,1)}), bf16[128,4,512]{2,0,1:T(8,128)(2,1)}, u32[]{:S(2)}, u32[]{:S(2)}) async-start(bf16[128,4,512]{2,0,1:T(8,128)(2,1)} %bitcast.217), calls=%async_computation | async-start | bytes 1048576 | tf_op jit(solution)/shard_map/all_to_all | solution.py:103
  81.3 2.6 fusion.151
  83.9 1.3 fusion.52
  85.2 0.4 fusion.51
  85.6 0.6 fusion.53
  86.2 0.2 stack.199
  86.4 0.7 reshape.96
  87.1 0.0 reduce-scatter.3.cloned.1.call-start
  87.1 9.2 %all-to-all-done = bf16[128,4,512]{2,0,1:T(8,128)(2,1)} async-done(((bf16[128,4,512]{2,0,1:T(8,128)(2,1)}), bf16[128,4,512]{2,0,1:T(8,128)(2,1)}, u32[]{:S(2)}, u32[]{:S(2)}) %all-to-all-start) | async-done | bytes 524320 | tf_op jit(solution)/shard_map/all_to_all | solution.py:103
  96.3 2.5 fusion.160
  98.8 0.9 copy.22
  99.7 3.5 %all-to-all-start.1 = ((bf16[128,4,512]{2,0,1:T(8,128)(2,1)}), bf16[128,4,512]{2,0,1:T(8,128)(2,1)S(1)}, u32[]{:S(2)}, u32[]{:S(2)}) async-start(bf16[128,4,512]{2,0,1:T(8,128)(2,1)} %bitcast.212), calls=%async_computation.2 | async-start | bytes 1048576 | tf_op jit(solution)/shard_map/all_to_all | solution.py:102
  103.2 0.0 reduce-scatter.5.cloned.1.call-start
  103.3 24.4 %all_gather.15 = bf16[512,512]{1,0:T(8,128)(2,1)S(1)} all-gather(bf16[128,512]{1,0:T(8,128)(2,1)S(1)} %copy-done.8), channel_id=1, replica_groups=mesh['dp'=8,'space'=4] {'space'}, dimensions={0}, use_global_device_ids=true | all-gather | bytes 655360 | tf_op jit(solution)/shard_map/all_gather | solution.py:99
  128.0 1.5 fusion.161
  129.6 1.3 collective-permute-start.3
  130.9 4.5 %collective-permute-start.2 = (bf16[3,16,512]{2,1,0:T(8,128)(2,1)S(1)}, bf16[3,16,512]{2,1,0:T(8,128)(2,1)S(1)}, u32[]{:S(2)}, u32[]{:S(2)}) collective-permute-start(bf16[3,16,512]{2,1,0:T(8,128)(2,1)S(1)} %bitcast.223), channel_id=1, source_target_pairs={{0,1},{1,2},{2,3},{4,5},{5,6},{6,7},{8,9},{9,10},{10,11},{12,13},{... | collective-permute-start | bytes 147464 | tf_op jit(solution)/shard_map/ppermute | solution.py:20
  135.5 39.2 %all-reduce.2 = (f32[512]{0:T(512)S(1)}, f32[512]{0:T(512)S(1)}, f32[512]{0:T(512)S(1)}) all-reduce(f32[512]{0:T(512)S(1)} %copy-done.71, f32[512]{0:T(512)S(1)} %copy-done.72, f32[512]{0:T(512)S(1)} %copy-done.70), channel_id=1, replica_groups=mesh['dp'=8,'space'=4] {'dp','space'}, use_global_device_ids=true, to_apply=%region_57.58 | all-reduce | flops 1536 | bytes 12288 | tf_op jit(solution)/shard_map/psum | solution.py:111
  174.7 0.6 broadcast_multiply_fusion.4
  175.3 0.6 broadcast_multiply_fusion.6
  176.2 2.1 fusion.141
  178.4 35.5 %all-reduce.5.cloned.1.call-done = f32[7,7,512]{2,1,0:T(8,128)} async-done(((f32[7,7,512]{2,1,0:T(8,128)}), f32[7,7,512]{2,1,0:T(8,128)}) %all-reduce.5.cloned.1.call-update) | async-done | bytes 100368 | tf_op jit(solution)/shard_map/psum | solution.py:111
  213.9 1.6 broadcast_multiply_fusion.2
  215.5 38.3 %reduce-scatter.3.cloned.1.call-done = f32[64,512]{1,0:T(8,128)} async-done(((f32[512,512]{1,0:T(8,128)}), f32[64,512]{1,0:T(8,128)}) %reduce-scatter.3.cloned.1.call-update) | async-done | bytes 131088 | tf_op jit(solution)/shard_map/reduce_scatter | solution.py:108
  253.8 1.6 broadcast_multiply_fusion.1
  255.4 37.4 %reduce-scatter.5.cloned.1.call-done = f32[512,64]{0,1:T(8,128)} async-done(((f32[512,512]{0,1:T(8,128)}), f32[512,64]{0,1:T(8,128)}) %reduce-scatter.5.cloned.1.call-update) | async-done | bytes 131088 | tf_op jit(solution)/shard_map/reduce_scatter | solution.py:109
  292.8 1.6 broadcast_multiply_fusion
  (165 shorter events, 0.5 us)
Async XLA Ops:
  7.2 34.3 %all-gather.3.cloned.1.call-start = ((), (), s32[]{:S(2)}) async-start(), calls=%async_computation.4 | async-start | bytes 2359296 | tf_op jit(solution)/shard_map/all_gather | solution.py:65
  7.9 62.2 %all-gather.5.cloned.1.call-start = ((), (), s32[]{:S(2)}) async-start(), calls=%async_computation.5 | async-start | bytes 2359296 | tf_op jit(solution)/shard_map/all_gather | solution.py:66
  9.5 10.4 %collective-permute-start.1 = (bf16[3,16,512]{2,1,0:T(8,128)(2,1)S(1)}, bf16[3,16,512]{2,1,0:T(8,128)(2,1)S(1)}, u32[]{:S(2)}, u32[]{:S(2)}) collective-permute-start(bf16[3,16,512]{2,1,0:T(8,128)(2,1)S(1)} %get-tuple-element.75), channel_id=1, source_target_pairs={{1,0},{2,1},{3,2},{5,4},{6,5},{7,6},{9,8},{10,9},{11,10},{13,12},{... | collective-permute-start | bytes 147464 | tf_op jit(solution)/shard_map/ppermute | solution.py:22
  10.8 9.2 %collective-permute-start = (bf16[3,16,512]{2,1,0:T(8,128)(2,1)S(1)}, bf16[3,16,512]{2,1,0:T(8,128)(2,1)S(1)}, u32[]{:S(2)}, u32[]{:S(2)}) collective-permute-start(bf16[3,16,512]{2,1,0:T(8,128)(2,1)S(1)} %get-tuple-element.74), channel_id=1, source_target_pairs={{0,1},{1,2},{2,3},{4,5},{5,6},{6,7},{8,9},{9,10},{10,11},{12,13},{... | collective-permute-start | bytes 147464 | tf_op jit(solution)/shard_map/ppermute | solution.py:20
  24.1 46.0 %copy-start.4 = (bf16[1,8,16,512]{3,2,1,0:T(8,128)(2,1)S(1)}, bf16[1,8,16,512]{3,2,1,0:T(8,128)(2,1)}, u32[]{:S(2)}) copy-start(bf16[1,8,16,512]{3,2,1,0:T(8,128)(2,1)} %param.8) | copy-start | bytes 393220
  24.1 46.0 %copy-start.5 = (bf16[1,8,16,512]{3,2,1,0:T(8,128)(2,1)S(1)}, bf16[1,8,16,512]{3,2,1,0:T(8,128)(2,1)}, u32[]{:S(2)}) copy-start(bf16[1,8,16,512]{3,2,1,0:T(8,128)(2,1)} %param.9) | copy-start | bytes 393220
  24.1 46.0 %copy-start.74 = (f32[512]{0:T(512)S(1)}, f32[512]{0:T(512)}, u32[]{:S(2)}) copy-start(f32[512]{0:T(512)} %param.13) | copy-start | bytes 6148
  76.7 19.6 %all-to-all-start = ((bf16[128,4,512]{2,0,1:T(8,128)(2,1)}), bf16[128,4,512]{2,0,1:T(8,128)(2,1)}, u32[]{:S(2)}, u32[]{:S(2)}) async-start(bf16[128,4,512]{2,0,1:T(8,128)(2,1)} %bitcast.217), calls=%async_computation | async-start | bytes 1048576 | tf_op jit(solution)/shard_map/all_to_all | solution.py:103
  81.3 132.6 %all-reduce.5.cloned.1.call-start = ((), (), s32[]{:S(2)}) async-start(), calls=%async_computation.8 | async-start | bytes 229376 | tf_op jit(solution)/shard_map/psum | solution.py:111
  87.1 166.7 %reduce-scatter.3.cloned.1.call-start = ((), (), s32[]{:S(2)}) async-start(), calls=%async_computation.6 | async-start | bytes 1179648 | tf_op jit(solution)/shard_map/reduce_scatter | solution.py:108
  99.7 28.3 %all-to-all-start.1 = ((bf16[128,4,512]{2,0,1:T(8,128)(2,1)}), bf16[128,4,512]{2,0,1:T(8,128)(2,1)S(1)}, u32[]{:S(2)}, u32[]{:S(2)}) async-start(bf16[128,4,512]{2,0,1:T(8,128)(2,1)} %bitcast.212), calls=%async_computation.2 | async-start | bytes 1048576 | tf_op jit(solution)/shard_map/all_to_all | solution.py:102
  103.2 32.2 %copy-start.70 = (f32[512]{0:T(512)S(1)}, f32[512]{0:T(512)}, u32[]{:S(2)}) copy-start(f32[512]{0:T(512)} %get-tuple-element.69) | copy-start | bytes 6148
  103.2 32.2 %copy-start.71 = (f32[512]{0:T(512)S(1)}, f32[512]{0:T(512)}, u32[]{:S(2)}) copy-start(f32[512]{0:T(512)} %get-tuple-element.57) | copy-start | bytes 6148
  103.2 32.2 %copy-start.72 = (f32[512]{0:T(512)S(1)}, f32[512]{0:T(512)}, u32[]{:S(2)}) copy-start(f32[512]{0:T(512)} %get-tuple-element.60) | copy-start | bytes 6148
  103.2 189.6 %reduce-scatter.5.cloned.1.call-start = ((), (), s32[]{:S(2)}) async-start(), calls=%async_computation.7 | async-start | bytes 1179648 | tf_op jit(solution)/shard_map/reduce_scatter | solution.py:109
  127.7 48.2 %copy-start.6 = (bf16[1,8,16,512]{3,2,1,0:T(8,128)(2,1)S(1)}, bf16[1,8,16,512]{3,2,1,0:T(8,128)(2,1)}, u32[]{:S(2)}) copy-start(bf16[1,8,16,512]{3,2,1,0:T(8,128)(2,1)} %param.9) | copy-start | bytes 393220
  127.7 48.2 %copy-start.11 = (f32[1,1,512]{2,1,0:T(1,128)S(1)}, f32[1,1,512]{2,1,0:T(1,128)}, u32[]{:S(2)}) copy-start(f32[1,1,512]{2,1,0:T(1,128)} %copy-done.10) | copy-start | bytes 6148
  127.7 48.2 %copy-start.13 = (f32[1,1,512]{2,1,0:T(1,128)S(1)}, f32[1,1,512]{2,1,0:T(1,128)}, u32[]{:S(2)}) copy-start(f32[1,1,512]{2,1,0:T(1,128)} %copy-done.12) | copy-start | bytes 6148
  127.7 48.2 %copy-start.15 = (f32[1,1,512]{2,1,0:T(1,128)S(1)}, f32[1,1,512]{2,1,0:T(1,128)}, u32[]{:S(2)}) copy-start(f32[1,1,512]{2,1,0:T(1,128)} %copy-done.14) | copy-start | bytes 6148
  127.7 48.2 %copy-start.17 = (f32[1,1,512]{2,1,0:T(1,128)S(1)}, f32[1,1,512]{2,1,0:T(1,128)}, u32[]{:S(2)}) copy-start(f32[1,1,512]{2,1,0:T(1,128)} %copy-done.16) | copy-start | bytes 6148
  127.7 48.2 %copy-start.19 = (f32[1,1,512]{2,1,0:T(1,128)S(1)}, f32[1,1,512]{2,1,0:T(1,128)}, u32[]{:S(2)}) copy-start(f32[1,1,512]{2,1,0:T(1,128)} %copy-done.18) | copy-start | bytes 6148
  127.8 48.2 %copy-start.21 = (f32[1,1,512]{2,1,0:T(1,128)S(1)}, f32[1,1,512]{2,1,0:T(1,128)}, u32[]{:S(2)}) copy-start(f32[1,1,512]{2,1,0:T(1,128)} %copy-done.20) | copy-start | bytes 6148
  127.8 48.2 %copy-start.23 = (f32[1,1,512]{2,1,0:T(1,128)S(1)}, f32[1,1,512]{2,1,0:T(1,128)}, u32[]{:S(2)}) copy-start(f32[1,1,512]{2,1,0:T(1,128)} %copy-done.22) | copy-start | bytes 6148
  127.8 48.2 %copy-start.25 = (f32[1,1,512]{2,1,0:T(1,128)S(1)}, f32[1,1,512]{2,1,0:T(1,128)}, u32[]{:S(2)}) copy-start(f32[1,1,512]{2,1,0:T(1,128)} %copy-done.24) | copy-start | bytes 6148
  127.8 48.2 %copy-start.27 = (f32[1,1,512]{2,1,0:T(1,128)S(1)}, f32[1,1,512]{2,1,0:T(1,128)}, u32[]{:S(2)}) copy-start(f32[1,1,512]{2,1,0:T(1,128)} %copy-done.26) | copy-start | bytes 6148
  127.8 48.2 %copy-start.29 = (f32[1,1,512]{2,1,0:T(1,128)S(1)}, f32[1,1,512]{2,1,0:T(1,128)}, u32[]{:S(2)}) copy-start(f32[1,1,512]{2,1,0:T(1,128)} %copy-done.28) | copy-start | bytes 6148
  127.8 48.2 %copy-start.31 = (f32[1,1,512]{2,1,0:T(1,128)S(1)}, f32[1,1,512]{2,1,0:T(1,128)}, u32[]{:S(2)}) copy-start(f32[1,1,512]{2,1,0:T(1,128)} %copy-done.30) | copy-start | bytes 6148
  127.8 48.2 %copy-start.33 = (f32[1,1,512]{2,1,0:T(1,128)S(1)}, f32[1,1,512]{2,1,0:T(1,128)}, u32[]{:S(2)}) copy-start(f32[1,1,512]{2,1,0:T(1,128)} %copy-done.32) | copy-start | bytes 6148
  127.8 48.2 %copy-start.35 = (f32[1,1,512]{2,1,0:T(1,128)S(1)}, f32[1,1,512]{2,1,0:T(1,128)}, u32[]{:S(2)}) copy-start(f32[1,1,512]{2,1,0:T(1,128)} %copy-done.34) | copy-start | bytes 6148
  127.8 48.2 %copy-start.37 = (f32[1,1,512]{2,1,0:T(1,128)S(1)}, f32[1,1,512]{2,1,0:T(1,128)}, u32[]{:S(2)}) copy-start(f32[1,1,512]{2,1,0:T(1,128)} %copy-done.36) | copy-start | bytes 6148
  127.8 48.2 %copy-start.39 = (f32[1,1,512]{2,1,0:T(1,128)S(1)}, f32[1,1,512]{2,1,0:T(1,128)}, u32[]{:S(2)}) copy-start(f32[1,1,512]{2,1,0:T(1,128)} %copy-done.38) | copy-start | bytes 6148
  127.9 48.2 %copy-start.41 = (f32[1,1,512]{2,1,0:T(1,128)S(1)}, f32[1,1,512]{2,1,0:T(1,128)}, u32[]{:S(2)}) copy-start(f32[1,1,512]{2,1,0:T(1,128)} %copy-done.40) | copy-start | bytes 6148
  127.9 48.2 %copy-start.43 = (f32[1,1,512]{2,1,0:T(1,128)S(1)}, f32[1,1,512]{2,1,0:T(1,128)}, u32[]{:S(2)}) copy-start(f32[1,1,512]{2,1,0:T(1,128)} %copy-done.42) | copy-start | bytes 6148
  127.9 48.2 %copy-start.45 = (f32[1,1,512]{2,1,0:T(1,128)S(1)}, f32[1,1,512]{2,1,0:T(1,128)}, u32[]{:S(2)}) copy-start(f32[1,1,512]{2,1,0:T(1,128)} %copy-done.44) | copy-start | bytes 6148
  127.9 48.2 %copy-start.47 = (f32[1,1,512]{2,1,0:T(1,128)S(1)}, f32[1,1,512]{2,1,0:T(1,128)}, u32[]{:S(2)}) copy-start(f32[1,1,512]{2,1,0:T(1,128)} %copy-done.46) | copy-start | bytes 6148
  127.9 48.2 %copy-start.49 = (f32[1,1,512]{2,1,0:T(1,128)S(1)}, f32[1,1,512]{2,1,0:T(1,128)}, u32[]{:S(2)}) copy-start(f32[1,1,512]{2,1,0:T(1,128)} %copy-done.48) | copy-start | bytes 6148
  127.9 48.2 %copy-start.51 = (f32[1,1,512]{2,1,0:T(1,128)S(1)}, f32[1,1,512]{2,1,0:T(1,128)}, u32[]{:S(2)}) copy-start(f32[1,1,512]{2,1,0:T(1,128)} %copy-done.50) | copy-start | bytes 6148
  127.9 48.2 %copy-start.53 = (f32[1,1,512]{2,1,0:T(1,128)S(1)}, f32[1,1,512]{2,1,0:T(1,128)}, u32[]{:S(2)}) copy-start(f32[1,1,512]{2,1,0:T(1,128)} %copy-done.52) | copy-start | bytes 6148
  127.9 48.2 %copy-start.55 = (f32[1,1,512]{2,1,0:T(1,128)S(1)}, f32[1,1,512]{2,1,0:T(1,128)}, u32[]{:S(2)}) copy-start(f32[1,1,512]{2,1,0:T(1,128)} %copy-done.54) | copy-start | bytes 6148
  127.9 48.2 %copy-start.57 = (f32[1,1,512]{2,1,0:T(1,128)S(1)}, f32[1,1,512]{2,1,0:T(1,128)}, u32[]{:S(2)}) copy-start(f32[1,1,512]{2,1,0:T(1,128)} %copy-done.56) | copy-start | bytes 6148
  127.9 48.2 %copy-start.59 = (f32[1,1,512]{2,1,0:T(1,128)S(1)}, f32[1,1,512]{2,1,0:T(1,128)}, u32[]{:S(2)}) copy-start(f32[1,1,512]{2,1,0:T(1,128)} %copy-done.58) | copy-start | bytes 6148
  128.0 48.2 %copy-start.61 = (f32[1,1,512]{2,1,0:T(1,128)S(1)}, f32[1,1,512]{2,1,0:T(1,128)}, u32[]{:S(2)}) copy-start(f32[1,1,512]{2,1,0:T(1,128)} %copy-done.60) | copy-start | bytes 6148
  128.0 48.2 %copy-start.63 = (f32[1,1,512]{2,1,0:T(1,128)S(1)}, f32[1,1,512]{2,1,0:T(1,128)}, u32[]{:S(2)}) copy-start(f32[1,1,512]{2,1,0:T(1,128)} %copy-done.62) | copy-start | bytes 6148
  128.0 48.2 %copy-start.65 = (f32[1,1,512]{2,1,0:T(1,128)S(1)}, f32[1,1,512]{2,1,0:T(1,128)}, u32[]{:S(2)}) copy-start(f32[1,1,512]{2,1,0:T(1,128)} %copy-done.64) | copy-start | bytes 6148
  128.0 48.2 %copy-start.67 = (f32[1,1,512]{2,1,0:T(1,128)S(1)}, f32[1,1,512]{2,1,0:T(1,128)}, u32[]{:S(2)}) copy-start(f32[1,1,512]{2,1,0:T(1,128)} %copy-done.66) | copy-start | bytes 6148
  128.0 48.2 %copy-start.69 = (f32[1,1,512]{2,1,0:T(1,128)S(1)}, f32[1,1,512]{2,1,0:T(1,128)}, u32[]{:S(2)}) copy-start(f32[1,1,512]{2,1,0:T(1,128)} %copy-done.68) | copy-start | bytes 6148
  129.6 46.3 %collective-permute-start.3 = (bf16[3,16,512]{2,1,0:T(8,128)(2,1)S(1)}, bf16[3,16,512]{2,1,0:T(8,128)(2,1)S(1)}, u32[]{:S(2)}, u32[]{:S(2)}) collective-permute-start(bf16[3,16,512]{2,1,0:T(8,128)(2,1)S(1)} %bitcast.224), channel_id=1, source_target_pairs={{1,0},{2,1},{3,2},{5,4},{6,5},{7,6},{9,8},{10,9},{11,10},{13,12},{... | collective-permute-start | bytes 147464 | tf_op jit(solution)/shard_map/ppermute | solution.py:22
  130.9 45.0 %collective-permute-start.2 = (bf16[3,16,512]{2,1,0:T(8,128)(2,1)S(1)}, bf16[3,16,512]{2,1,0:T(8,128)(2,1)S(1)}, u32[]{:S(2)}, u32[]{:S(2)}) collective-permute-start(bf16[3,16,512]{2,1,0:T(8,128)(2,1)S(1)} %bitcast.223), channel_id=1, source_target_pairs={{0,1},{1,2},{2,3},{4,5},{5,6},{6,7},{8,9},{9,10},{10,11},{12,13},{... | collective-permute-start | bytes 147464 | tf_op jit(solution)/shard_map/ppermute | solution.py:20
  (38 other events, 198.1 us)
Sparse Core Ops, SparseCore 0:
  9.9 30.4 all-gather.2
  42.3 27.7 all-gather.4
  88.3 125.6 all-reduce.4
  216.9 36.7 reduce-scatter.2
  256.8 35.9 reduce-scatter.4
where the time goes:
time: 302 us; the launch traced here: 301 us
  waiting for transfers between devices  148 us (49%)
  blocking collectives  81 us (27%)
  starting transfers between devices  20.9 us (7%)
  between operations  15 us (5%)
  other arithmetic  13.5 us (4%)
  matrix products  13 us (4%)
  local copies, waits for them, and re-layouts  9.06 us (3%)
    psum x1, blocking collectives, local(): lax.psum((kernel_grad(padded, d_grid), jnp.sum(d_norm * scaled_rows, axis...  39.2 us
    reduce_scatter x1, waiting for transfers between devices, local(): lax.psum_scatter(up_part, 'dp', scatter_dimension=0, tiled=True)  38.3 us
    reduce_scatter x1, waiting for transfers between devices, local(): lax.psum_scatter(down_part, 'dp', scatter_dimension=1, tiled=True)  37.4 us
    psum x1, waiting for transfers between devices, local(): lax.psum((kernel_grad(padded, d_grid), jnp.sum(d_norm * scaled_rows, axis...  35.5 us
    all_gather x1, waiting for transfers between devices, local(): lax.all_gather(w_down, 'dp', axis=0, tiled=True)  26.5 us
    all_gather x1, blocking collectives, local(): lax.all_gather(d_mixed, 'space', axis=0, tiled=True)  24.4 us
    all_gather x1, blocking collectives, local(): lax.all_gather(tokens, 'space', axis=0, tiled=True)  17.3 us
    ppermute x2, starting transfers between devices, extended_2(): lax.ppermute(tail, axis, [(i, (i + 1) % count) for i in range(ends)])  10.1 us
  transfers between devices with their start and end apart: 11, of which 5 were waited for; matrix products, arithmetic and copies ran while one was open for 9% of the time, Pallas kernels for 0%

commit v1 on v0

v1 whole, which is shorter than its diff:
```python
import functools
import math

import jax
import jax.numpy as jnp
from jax import lax
from jax.experimental import pallas as pl
from jax.experimental.pallas import tpu as pltpu
from jax.sharding import PartitionSpec as P

F32, BF16 = jnp.float32, jnp.bfloat16
LANES = 128
EDGE = 8


def gelu_pair(preact):
    cumulative = 0.5 * (1.0 + lax.erf(preact * (1.0 / math.sqrt(2.0))))
    density = jnp.exp(-0.5 * preact * preact) * (1.0 / math.sqrt(2.0 * math.pi))
    return (preact * cumulative, cumulative + preact * density)


def remote(src, dst, send_sem, recv_sem, device):
    return pltpu.make_async_remote_copy(
        src_ref=src,
        dst_ref=dst,
        send_sem=send_sem,
        recv_sem=recv_sem,
        device_id=device,
        device_id_type=pl.DeviceIdType.MESH,
    )


def block_kernel(
    sizes,
    x_ref, cot_ref, kern_ref, gain_ref, bias_ref, scale_ref, wup_ref, wdown_ref,
    res_ref, dfeat_ref, gup_ref, gdown_ref, small_ref,
    xpad, gpad, halo_x, halo_g, conv, scaled_ref, dconv, upg, tok, dmx, hid, dpre,
    part_n, part_m, r1n, r1m, chip_n, chip_m, r2n, r2m, own_n, own_m,
    gpart, gsend, grecv, fsend, frecv, small, ar1, ar2, ar3,
    hx_s, hx_r, hg_s, hg_r, w_s, w_r, dm_s, dm_r, tk_s, tk_r,
    an_s, an_r, am_s, am_r, bn_s, bn_r, bm_s, bm_r,
    gz_s, gz_r, fi_s, fi_r, s1_s, s1_r, s2_s, s2_r, s3_s, s3_r,
):
    n_dp, n_sp, rows, cols, width, taps = sizes
    chips, share = n_dp // 2, n_dp // n_sp
    margin = taps // 2
    pixels = rows * cols
    hidden = wdown_ref.shape[0]
    d, s = lax.axis_index("dp"), lax.axis_index("space")
    chip, core = d // 2, lax.rem(d, 2)
    sibling = chip * 2 + (1 - core)
    home = d // share
    place = lax.rem(d, share)
    inside = (home == s).astype(jnp.int32)

    def dp_peer(off):
        return lax.rem(d + off, n_dp)

    def sp_peer(off):
        return lax.rem(s + off, n_sp)

    barrier = pltpu.get_barrier_semaphore()

    def greet(device):
        pl.semaphore_signal(barrier, inc=1, device_id=device, device_id_type=pl.DeviceIdType.MESH)

    for off in range(1, n_dp):
        greet((dp_peer(off), s))
    for off in range(1, n_sp):
        greet((d, sp_peer(off)))
    for b in range(share):
        own_block = jnp.logical_and(home == s, place == b)

        @pl.when(jnp.logical_not(own_block))
        def _():
            greet((s * share + b, home))

    dmx[d] = (scale_ref[...] * cot_ref[...].astype(F32)).astype(BF16)
    pl.semaphore_wait(barrier, (n_dp - 1) + (n_sp - 1) + share - inside)

    has_up, has_down = s > 0, s < n_sp - 1

    def halo_copies(source, halo, send, recv):
        down = remote(source.at[pl.ds(rows - margin, margin)], halo.at[0], send.at[0], recv.at[0], (d, jnp.minimum(s + 1, n_sp - 1)))
        up = remote(source.at[pl.ds(0, margin)], halo.at[1], send.at[1], recv.at[1], (d, jnp.maximum(s - 1, 0)))
        return down, up

    def halo_start(copies):
        pl.when(has_down)(copies[0].start)
        pl.when(has_up)(copies[1].start)

    def halo_land(copies, halo, padded):
        @pl.when(has_up)
        def _():
            copies[0].wait_recv()
            padded[0:margin, EDGE:EDGE + cols] = halo[0].astype(F32)

        @pl.when(has_down)
        def _():
            copies[1].wait_recv()
            padded[rows + margin:, EDGE:EDGE + cols] = halo[1].astype(F32)

    def halo_sent(copies):
        pl.when(has_down)(copies[0].wait_send)
        pl.when(has_up)(copies[1].wait_send)

    hx = halo_copies(x_ref, halo_x, hx_s, hx_r)
    halo_start(hx)

    def spread(buf, send, recv):
        first = [remote(buf.at[d], buf.at[d], send.at[0], recv.at[d], (sibling, s))]
        for off in range(1, chips):
            first.append(remote(buf.at[d], buf.at[d], send.at[off], recv.at[d], (lax.rem(chip + off, chips) * 2 + core, s)))
        passed = []
        for off in range(1, chips):
            slot = lax.rem(chip + chips - off, chips) * 2 + core
            passed.append(remote(buf.at[slot], buf.at[slot], send.at[chips - 1 + off], recv.at[slot], (sibling, s)))
        last = []
        for off in range(chips):
            slot = lax.rem(chip + chips - off, chips) * 2 + (1 - core)
            last.append(remote(buf.at[slot], buf.at[slot], send.at[0], recv.at[slot], (sibling, s)))
        return first, passed, last

    dm_first, dm_passed, dm_last = spread(dmx, dm_s, dm_r)
    w_out = [remote(wup_ref.at[dp_peer(off)], upg.at[d], w_s.at[off], w_r.at[d], (dp_peer(off), s)) for off in range(1, n_dp)]
    w_in = [remote(wup_ref.at[dp_peer(off)], upg.at[dp_peer(off)], w_s.at[off], w_r.at[dp_peer(off)], (sibling, s)) for off in range(1, n_dp)]
    for copy in w_out:
        copy.start()
    for copy in dm_first:
        copy.start()
    upg[d] = wup_ref[d]

    wide = xpad.shape[1]
    for padded in (xpad, gpad):
        padded[...] = jnp.zeros(padded.shape, F32)
    xpad[margin:margin + rows, EDGE:EDGE + cols] = x_ref[...].astype(F32)
    halo_land(hx, halo_x, xpad)

    def convolve(padded, flip, lanes):
        total = jnp.zeros((rows, cols, LANES), F32)
        for b in range(taps):
            first = EDGE - margin + b
            window = padded[:, first:first + cols, lanes]
            for a in range(taps):
                tap = a * taps + b
                tap = taps * taps - 1 - tap if flip else tap
                total = total + kern_ref[tap:tap + 1, lanes].reshape(1, 1, LANES) * window[a:a + rows]
        return total

    def lanes_of(c):
        return pl.ds(pl.multiple_of(c * LANES, LANES), LANES)

    @pl.loop(0, width // LANES)
    def _(c):
        conv[:, lanes_of(c)] = convolve(xpad, False, lanes_of(c)).reshape(pixels, LANES)

    center = conv[...]
    center = center - jnp.mean(center, axis=-1, keepdims=True)
    inverse = lax.rsqrt(jnp.mean(center * center, axis=-1, keepdims=True) + 1e-06)
    normal = center * inverse
    scaled_ref[...] = normal
    tok[d] = (normal * gain_ref[...] + bias_ref[...]).astype(BF16)

    tk_first, tk_passed, tk_last = spread(tok, tk_s, tk_r)
    for copy in tk_first:
        copy.start()
    for group in (dm_passed, tk_passed):
        for copy in group:
            copy.wait_recv()
            copy.start()
    for copy in w_in:
        copy.wait_recv()
    for group in (dm_last, tk_last):
        for copy in group:
            copy.wait_recv()

    def nn(a, b):
        return lax.dot_general(a, b, (((1,), (0,)), ((), ())), preferred_element_type=F32)

    def nt(a, b):
        return lax.dot_general(a, b, (((1,), (1,)), ((), ())), preferred_element_type=F32)

    def tn(a, b):
        return lax.dot_general(a, b, (((0,), (0,)), ((), ())), preferred_element_type=F32)

    def cross(kind, to):
        buf, got, send, recv = kind
        return remote(buf.at[to], got.at[to], send.at[to], recv.at[to], (sibling, s))

    def home_copy(kind, to):
        buf, got, send, recv = kind
        return remote(buf.at[to], got.at[chip], send.at[to], recv.at[chip], (to * 2 + core, s))

    cross_n, cross_m = (part_n, r1n, an_s, an_r), (part_m, r1m, am_s, am_r)
    home_n, home_m = (chip_n, r2n, bn_s, bn_r), (chip_m, r2m, bm_s, bm_r)

    def products(slot):
        up = upg[...].reshape(width, hidden)
        activation, slope = gelu_pair(nn(tok[slot], up))
        act = activation.astype(BF16)
        grad = (nt(dmx[slot], wdown_ref[...]) * slope).astype(BF16)
        hid[slot] = act
        dpre[slot] = grad
        return nt(grad, up), nn(act, wdown_ref[...])

    @pl.loop(0, chips)
    def _(i):
        to = lax.rem(chip + 1 + i, chips)
        normed, mixed = products(to * 2 + (1 - core))
        part_n[to] = normed.astype(BF16)
        cross(cross_n, to).start()
        part_m[to] = mixed.astype(BF16)
        cross(cross_m, to).start()

    @pl.loop(0, chips - 1)
    def _(i):
        to = lax.rem(chip + 1 + i, chips)
        normed, mixed = products(to * 2 + core)
        cross(cross_n, to).wait_recv()
        chip_n[to] = (normed + r1n[to].astype(F32)).astype(BF16)
        home_copy(home_n, to).start()
        cross(cross_m, to).wait_recv()
        chip_m[to] = (mixed + r1m[to].astype(F32)).astype(BF16)
        home_copy(home_m, to).start()

    normed, mixed = products(d)
    cross(cross_n, chip).wait_recv()
    own_n[...] = normed + r1n[chip].astype(F32)
    cross(cross_m, chip).wait_recv()
    own_m[...] = mixed + r1m[chip].astype(F32)

    strip = width // n_sp
    part_rows = strip // share
    flat = (n_dp * pixels,)
    for which, (left, right) in enumerate(((tok, dpre), (dmx, hid))):
        gpart[which] = tn(left[...].reshape(flat + (width,)), right[...].reshape(flat + (hidden,)))
        for k in range(n_sp):
            gsend[k, which] = gpart[which, k * strip:(k + 1) * strip].astype(BF16)
    gz_out = [remote(gsend.at[sp_peer(off)], grecv.at[s], gz_s.at[off], gz_r.at[s], (d, sp_peer(off))) for off in range(1, n_sp)]
    gz_in = [remote(gsend.at[sp_peer(off)], grecv.at[sp_peer(off)], gz_s.at[off], gz_r.at[sp_peer(off)], (d, sp_peer(off))) for off in range(1, n_sp)]
    for copy in gz_out:
        copy.start()

    def arrive(got, send, recv, own):
        total = own[...]
        for off in range(1, chips):
            source = lax.rem(chip + off, chips)
            remote(got.at[source], got.at[source], send.at[source], recv.at[source], (sibling, s)).wait_recv()
            total = total + got[source].astype(F32)
        return total

    d_norm = arrive(r2n, bn_s, bn_r, own_n)
    normal = scaled_ref[...]
    d_hat = d_norm * gain_ref[...]
    lead = jnp.mean(d_hat, axis=-1, keepdims=True)
    second = jnp.mean(d_hat * normal, axis=-1, keepdims=True)
    dconv[...] = (inverse * (d_hat - lead - normal * second)).astype(BF16).reshape(rows, cols, width)
    hg = halo_copies(dconv, halo_g, hg_s, hg_r)
    halo_start(hg)
    gpad[margin:margin + rows, EDGE:EDGE + cols] = dconv[...].astype(F32)

    per = small.shape[1]
    count = taps * taps

    def put(row, lanes, value):
        small[row // per, row % per:row % per + 1, lanes] = value

    small[...] = jnp.zeros(small.shape, F32)
    everything = slice(None)
    put(count, everything, jnp.sum(d_norm * normal, axis=0, keepdims=True))
    put(count + 1, everything, jnp.sum(d_norm, axis=0, keepdims=True))

    @pl.loop(0, width // LANES)
    def _(c):
        lanes = lanes_of(c)
        upstream = gpad[margin:margin + rows, EDGE:EDGE + cols, lanes]
        for b in range(taps):
            first = EDGE - margin + b
            window = xpad[:, first:first + cols, lanes]
            for a in range(taps):
                product = jnp.sum(window[a:a + rows] * upstream, axis=0)
                put(a * taps + b, lanes, jnp.sum(product, axis=0, keepdims=True))

    mixed = arrive(r2m, bm_s, bm_r, own_m)
    res_ref[...] = (x_ref[...].reshape(pixels, width).astype(F32) + scale_ref[...] * mixed).astype(BF16).reshape(rows, cols, width)
    put(count + 2, everything, jnp.sum(cot_ref[...].astype(F32) * mixed, axis=0, keepdims=True))

    s1_out = [remote(small.at[dp_peer(off)], ar1.at[d], s1_s.at[off], s1_r.at[d], (dp_peer(off), s)) for off in range(1, n_dp)]
    s1_in = [remote(small.at[dp_peer(off)], ar1.at[dp_peer(off)], s1_s.at[off], s1_r.at[dp_peer(off)], (sibling, s)) for off in range(1, n_dp)]
    for copy in s1_out:
        copy.start()
    ar1[d] = small[d]

    for copy in gz_in:
        copy.wait_recv()
    for which in range(2):
        total = gpart[which, pl.ds(pl.multiple_of(s * strip, strip), strip)]
        for off in range(1, n_sp):
            total = total + grecv[sp_peer(off), which].astype(F32)
        for b in range(share):
            fsend[b, which] = total[b * part_rows:(b + 1) * part_rows].astype(BF16)
    for b in range(share):
        own_block = jnp.logical_and(home == s, place == b)
        copy = remote(fsend.at[b], frecv.at[place], fi_s.at[b], fi_r.at[place], (s * share + b, home))

        pl.when(jnp.logical_not(own_block))(copy.start)

        @pl.when(own_block)
        def _():
            frecv[b] = fsend[b]

    for copy in s1_in:
        copy.wait_recv()
    ar2[s] = jnp.sum(ar1[...], axis=0)
    s2_out = [remote(ar2.at[s], ar2.at[s], s2_s.at[off], s2_r.at[s], (d, sp_peer(off))) for off in range(1, n_sp)]
    s2_in = [remote(ar2.at[s], ar2.at[sp_peer(off)], s2_s.at[off], s2_r.at[sp_peer(off)], (d, sp_peer(off))) for off in range(1, n_sp)]
    for copy in s2_out:
        copy.start()

    halo_land(hg, halo_g, gpad)

    @pl.loop(0, width // LANES)
    def _(c):
        lanes = lanes_of(c)
        cot = cot_ref[:, lanes].astype(F32).reshape(rows, cols, LANES)
        dfeat_ref[:, :, lanes] = cot + convolve(gpad, True, lanes)

    for copy in s2_in:
        copy.wait_recv()
    ar3[d] = jnp.sum(ar2[...], axis=0)
    s3_out = [remote(ar3.at[d], ar3.at[d], s3_s.at[off], s3_r.at[d], (dp_peer(off), s)) for off in range(1, n_dp)]
    s3_in = [remote(ar3.at[d], ar3.at[dp_peer(off)], s3_s.at[off], s3_r.at[dp_peer(off)], (sibling, s)) for off in range(1, n_dp)]
    for copy in s3_out:
        copy.start()

    for b in range(share):
        own_block = jnp.logical_and(home == s, place == b)
        copy = remote(fsend.at[b], frecv.at[b], fi_s.at[b], fi_r.at[b], (s * share + b, home))
        pl.when(jnp.logical_not(own_block))(copy.wait_recv)
    for b in range(share):
        gup_ref[:, b * hidden:(b + 1) * hidden] = frecv[b, 0].astype(F32)
        gdown_ref[:, b * hidden:(b + 1) * hidden] = frecv[b, 1].astype(F32)

    for copy in s3_in:
        copy.wait_recv()
    small_ref[...] = ar3[...]

    halo_sent(hx)
    halo_sent(hg)
    for group in (w_out, dm_first, dm_passed, tk_first, tk_passed, gz_out, s1_out, s2_out, s3_out):
        for copy in group:
            copy.wait_send()
    for b in range(share):
        own_block = jnp.logical_and(home == s, place == b)
        copy = remote(fsend.at[b], frecv.at[b], fi_s.at[b], fi_r.at[b], (s * share + b, home))
        pl.when(jnp.logical_not(own_block))(copy.wait_send)

    for off in range(chips):
        to = lax.rem(chip + 1 + off, chips)
        cross(cross_n, to).wait_send()
        cross(cross_m, to).wait_send()
        if off < chips - 1:
            home_copy(home_n, to).wait_send()
            home_copy(home_m, to).wait_send()


def local(features, cotangent, dw_kernel, ln_gain, ln_bias, layer_scale, w_up, w_down):
    n_dp, n_sp = lax.axis_size("dp"), lax.axis_size("space")
    _, rows, cols, width = features.shape
    taps = dw_kernel.shape[0]
    margin = taps // 2
    pixels = rows * cols
    hidden = w_down.shape[0]
    chips, share = n_dp // 2, n_dp // n_sp
    strip = width // n_sp
    part_rows = strip // share
    count = taps * taps
    per = -(-(count + 3) // n_dp)
    outgoing = w_up.reshape(w_up.shape[0], n_dp, hidden).transpose(1, 0, 2)
    padded = (rows + 2 * margin, cols + 2 * EDGE, width)
    dma = lambda k: pltpu.SemaphoreType.DMA((k,))
    vm = pltpu.VMEM
    scratch = [
        vm(padded, F32), vm(padded, F32),
        vm((2, margin, cols, width), BF16), vm((2, margin, cols, width), BF16),
        vm((pixels, width), F32), vm((pixels, width), F32), vm((rows, cols, width), BF16),
        vm(outgoing.shape, BF16),
        vm((n_dp, pixels, width), BF16), vm((n_dp, pixels, width), BF16),
        vm((n_dp, pixels, hidden), BF16), vm((n_dp, pixels, hidden), BF16),
    ]
    scratch += [vm((chips, pixels, width), BF16)] * 8
    scratch += [vm((pixels, width), F32)] * 2
    scratch += [
        vm((2, width, hidden), F32),
        vm((n_sp, 2, strip, hidden), BF16), vm((n_sp, 2, strip, hidden), BF16),
        vm((share, 2, part_rows, hidden), BF16), vm((share, 2, part_rows, hidden), BF16),
        vm((n_dp, per, width), F32), vm((n_dp, per, width), F32),
        vm((n_sp, per, width), F32), vm((n_dp, per, width), F32),
    ]
    scratch += [dma(2)] * 4 + [dma(n_dp)] * 6 + [dma(chips)] * 8
    scratch += [dma(n_sp)] * 2 + [dma(share)] * 2 + [dma(n_dp)] * 2 + [dma(n_sp)] * 2 + [dma(n_dp)] * 2
    whole = pl.BlockSpec(memory_space=pltpu.VMEM)
    result, d_feat, grad_up, grad_down, small = pl.pallas_call(
        functools.partial(block_kernel, (n_dp, n_sp, rows, cols, width, taps)),
        out_shape=(
            jax.ShapeDtypeStruct((rows, cols, width), BF16),
            jax.ShapeDtypeStruct((rows, cols, width), F32),
            jax.ShapeDtypeStruct((part_rows, share * hidden), F32),
            jax.ShapeDtypeStruct((part_rows, share * hidden), F32),
            jax.ShapeDtypeStruct((n_dp, per, width), F32),
        ),
        in_specs=[whole] * 8,
        out_specs=(whole,) * 5,
        scratch_shapes=scratch,
        compiler_params=pltpu.CompilerParams(
            collective_id=0, has_side_effects=True, vmem_limit_bytes=60 << 20
        ),
    )(
        features[0],
        cotangent[0].reshape(pixels, width),
        dw_kernel.reshape(count, width),
        ln_gain.reshape(1, width),
        ln_bias.reshape(1, width),
        layer_scale.reshape(1, width),
        outgoing,
        w_down,
    )
    regions = float(n_dp)
    small = small.reshape(n_dp * per, width) / regions
    return (
        result[None],
        d_feat[None],
        grad_up / regions,
        grad_down.T / regions,
        small[:count].reshape(taps, taps, width),
        small[count],
        small[count + 1],
        small[count + 2],
    )


def solution(mesh):
    in_specs = (
        P("dp", "space", None, None),
        P("dp", "space", None, None),
        P(),
        P(),
        P(),
        P(),
        P("dp", None),
        P("dp", None),
    )
    out_specs = (
        P("dp", "space", None, None),
        P("dp", "space", None, None),
        P("dp", "space"),
        P("space", "dp"),
        P(),
        P(),
        P(),
        P(),
    )
    return jax.shard_map(local, mesh=mesh, in_specs=in_specs, out_specs=out_specs, check_vma=False)
```

time: 302 us -> 65.8 us (0.22)
  waiting for transfers between devices: 148 us -> 0 us
  blocking collectives: 81 us -> 0 us
  Pallas kernels: 0 us -> 57.1 us
  starting transfers between devices: 20.9 us -> 0 us
  between operations: 15 us -> 0.67 us
  matrix products: 13 us -> 0 us
  other arithmetic: 13.5 us -> 1.64 us
    reduce_scatter x2 -> x0, waiting for transfers between devices: 75.8 us -> none  [the longest x1 38.3 us: local(): lax.psum_scatter(up_part, 'dp', scatter_dimension=0, tiled=True)]
    pallas_call x0 -> x1, Pallas kernels: none -> 57.1 us  [local(): pl.pallas_call(functools.partial(block_kernel, (n_dp, n_sp, rows, cols, w...]
    all_gather x2 -> x0, blocking collectives: 41.7 us -> none  [the longest x1 24.4 us: local(): lax.all_gather(d_mixed, 'space', axis=0, tiled=True)]
    psum x1 -> x0, blocking collectives: 39.2 us -> none  [local(): lax.psum((kernel_grad(padded, d_grid), jnp.sum(d_norm * scaled_rows, axis...]
    psum x1 -> x0, waiting for transfers between devices: 35.5 us -> none  [local(): lax.psum((kernel_grad(padded, d_grid), jnp.sum(d_norm * scaled_rows, axis...]
    all_gather x2 -> x0, waiting for transfers between devices: 26.5 us -> none  [the longest x1 26.5 us: local(): lax.all_gather(w_down, 'dp', axis=0, tiled=True)]
    dot_general x6 -> x0, matrix products: 13 us -> none  [the longest x1 3.45 us: local(): mixed = jnp.dot(hidden_act, down_full, preferred_element_type=jnp.float32)]
    ppermute x4 -> x0, starting transfers between devices: 12.7 us -> none  [the longest x2 10.1 us: extended_2(): lax.ppermute(tail, axis, [(i, (i + 1) % count) for i in range(ends)])]
  transfers between devices with their start and end apart: 11 -> 0, of which waited for: 5 -> 0; matrix products, arithmetic and copies ran while one was open for 9% -> 0% of each run, Pallas kernels for 0% -> 0%
where the time goes in v1:
time: 65.8 us; the launch traced here: 65.6 us
  Pallas kernels  57.1 us (87%)
  local copies, waits for them, and re-layouts  6.17 us (9%)
  other arithmetic  1.64 us (2%)
  between operations  0.67 us (1%)
    pallas_call x1, Pallas kernels, local(): pl.pallas_call(functools.partial(block_kernel, (n_dp, n_sp, rows, cols, w...  57.1 us
    unnamed x10, local copies, waits for them, and re-layouts  1.68 us
    reshape x1, local copies, waits for them, and re-layouts, local(): outgoing = w_up.reshape(w_up.shape[0], n_dp, hidden).transpose(1, 0, 2)  1.67 us
    reshape x1, local copies, waits for them, and re-layouts, local(): dw_kernel.reshape(count, width)  1.56 us

profile of v1, /device:TPU:0, one launch (start us, length us, event | category | flops | bytes accessed | tf_op | source)
XLA Modules:
  0.0 65.6 jit_solution(1661184455801376562)
XLA Ops:
  0.6 1.6 %reshape.37.kern_ref = f32[49,512]{1,0:T(8,128)} reshape(f32[7,7,512]{2,1,0:T(8,128)} %param.10) | data formatting | bytes 200704 | tf_op jit(solution)/shard_map/reshape | solution.py:421
  2.2 1.7 %copy.19 = bf16[8,8,8,256]{3,2,0,1:T(8,128)(2,1)} copy(bf16[8,8,8,256]{3,2,1,0:T(8,128)(2,1)} %bitcast.20) | data formatting | bytes 524288 | tf_op jit(solution)/shard_map/reshape | solution.py:379
  3.9 57.1 %shard_map.143 = (bf16[8,16,512]{2,1,0:T(8,128)(2,1)}, f32[8,16,512]{2,1,0:T(8,128)}, f32[64,512]{1,0:T(8,128)}, f32[64,512]{1,0:T(8,128)}, f32[8,7,512]{2,1,0:T(8,128)}) custom-call(bf16[8,16,512]{2,1,0:T(8,128)(2,1)} %bitcast.22, bf16[128,512]{1,0:T(8,128)(2,1)} %bitcast.23, f32[49,512]{1,0:T(8,128)} %reshape.37.kern_ref, f32[1,512]{1,0:T(1,128)} %bitcast.25, ...), custom_call_target="tpu_custom_call" | custom-call | tf_op jit(solution)/shard_map/pallas_call | solution.py:403
  61.0 0.9 %broadcast_multiply_fusion = f32[8,7,512]{2,1,0:T(8,128)S(1)} fusion(f32[8,7,512]{2,1,0:T(8,128)} %get-tuple-element.17), kind=kLoop, calls=%fused_computation.2 | loop fusion | flops 28672 | bytes 229376 | tf_op jit(solution)/shard_map/div | solution.py:429
  61.9 0.0 copy-start.3
  61.9 0.0 copy-start.2
  61.9 0.6 fusion
  62.5 0.7 slice.17
  63.2 0.0 copy-done.3
  63.2 0.0 copy-done.2
  63.2 0.0 copy-start.1
  63.2 0.7 %multiply_bitcast_fusion = (f32[512,64]{0,1:T(8,128)}, f32[64,512]{1,0:T(8,128)}) fusion(f32[64,512]{1,0:T(8,128)S(1)} %copy-done.3, f32[64,512]{1,0:T(8,128)S(1)} %copy-done.2), kind=kLoop, calls=%fused_computation.1 | loop fusion | flops 65536 | bytes 524288 | tf_op jit(solution)/shard_map/div | solution.py:434
  63.9 0.0 copy-start
  63.9 0.2 copy-done.1
  64.1 0.7 copy.22
  64.8 0.1 copy-done
  64.9 0.7 %copy.23 = f32[1,8,16,512]{3,2,1,0:T(8,128)} copy(f32[1,8,16,512]{3,2,1,0:T(8,128)S(1)} %bitcast.21) | data formatting | bytes 524288
  (1 shorter events, 0.0 us)
Async XLA Ops:
  61.9 1.3 %copy-start.3 = (f32[64,512]{1,0:T(8,128)S(1)}, f32[64,512]{1,0:T(8,128)}, u32[]{:S(2)}) copy-start(f32[64,512]{1,0:T(8,128)} %get-tuple-element.16) | copy-start | bytes 393220
  61.9 1.3 %copy-start.2 = (f32[64,512]{1,0:T(8,128)S(1)}, f32[64,512]{1,0:T(8,128)}, u32[]{:S(2)}) copy-start(f32[64,512]{1,0:T(8,128)} %get-tuple-element.15) | copy-start | bytes 393220
  63.2 1.0 %copy-start.1 = (bf16[8,16,512]{2,1,0:T(8,128)(2,1)S(1)}, bf16[8,16,512]{2,1,0:T(8,128)(2,1)}, u32[]{:S(2)}) copy-start(bf16[8,16,512]{2,1,0:T(8,128)(2,1)} %get-tuple-element.13) | copy-start | bytes 393220
  63.9 1.0 %copy-start = (f32[8,16,512]{2,1,0:T(8,128)S(1)}, f32[8,16,512]{2,1,0:T(8,128)}, u32[]{:S(2)}) copy-start(f32[8,16,512]{2,1,0:T(8,128)} %get-tuple-element.14) | copy-start | bytes 786436

commit v2 on v1

--- a/solution.py
+++ b/solution.py
@@ -33,13 +33,13 @@
 def block_kernel(
     sizes,
     x_ref, cot_ref, kern_ref, gain_ref, bias_ref, scale_ref, wup_ref, wdown_ref,
-    res_ref, dfeat_ref, gup_ref, gdown_ref, small_ref,
-    xpad, gpad, halo_x, halo_g, conv, scaled_ref, dconv, upg, tok, dmx, hid, dpre,
+    res_ref, dfeat_ref, gup_ref, gdown_ref, gkern_ref, ggain_ref, gbias_ref, gscale_ref,
+    xpad, gpad, halo_x, halo_g, conv, scaled_ref, dconv, wout, upg, tok, dmx, hid, dpre,
     part_n, part_m, r1n, r1m, chip_n, chip_m, r2n, r2m, own_n, own_m,
-    gpart, gsend, grecv, fsend, frecv, small, ar1, ar2, ar3,
+    gsend, grecv, dscale, small, ar1, ar2, ar3,
     hx_s, hx_r, hg_s, hg_r, w_s, w_r, dm_s, dm_r, tk_s, tk_r,
     an_s, an_r, am_s, am_r, bn_s, bn_r, bm_s, bm_r,
-    gz_s, gz_r, fi_s, fi_r, s1_s, s1_r, s2_s, s2_r, s3_s, s3_r,
+    gz_s, gz_r, s1_s, s1_r, s2_s, s2_r, s3_s, s3_r,
 ):
     n_dp, n_sp, rows, cols, width, taps = sizes
     chips, share = n_dp // 2, n_dp // n_sp
@@ -53,6 +53,9 @@
     place = lax.rem(d, share)
     inside = (home == s).astype(jnp.int32)
 
+    def is_self(j, k):
+        return jnp.logical_and(jnp.logical_and(home == s, place == j), s == k)
+
     def dp_peer(off):
         return lax.rem(d + off, n_dp)
 
@@ -68,15 +71,22 @@
         greet((dp_peer(off), s))
     for off in range(1, n_sp):
         greet((d, sp_peer(off)))
-    for b in range(share):
-        own_block = jnp.logical_and(home == s, place == b)
-
-        @pl.when(jnp.logical_not(own_block))
-        def _():
-            greet((s * share + b, home))
+    for j in range(share):
+        for k in range(n_sp):
+            @pl.when(jnp.logical_not(is_self(j, k)))
+            def _():
+                greet((s * share + j, jnp.int32(k)))
 
     dmx[d] = (scale_ref[...] * cot_ref[...].astype(F32)).astype(BF16)
-    pl.semaphore_wait(barrier, (n_dp - 1) + (n_sp - 1) + share - inside)
+    for t in range(n_dp):
+        wout[t] = wup_ref[:, t * hidden:(t + 1) * hidden]
+    upg[d] = wout[d]
+    for padded in (xpad, gpad):
+        padded[...] = jnp.zeros(padded.shape, F32)
+    xpad[margin:margin + rows, EDGE:EDGE + cols] = x_ref[...].astype(F32)
+    dscale[...] = jnp.zeros(dscale.shape, F32)
+    small[...] = jnp.zeros(small.shape, F32)
+    pl.semaphore_wait(barrier, (n_dp - 1) + (n_sp - 1) + n_dp - inside)
 
     has_up, has_down = s > 0, s < n_sp - 1
 
@@ -122,18 +132,13 @@
         return first, passed, last
 
     dm_first, dm_passed, dm_last = spread(dmx, dm_s, dm_r)
-    w_out = [remote(wup_ref.at[dp_peer(off)], upg.at[d], w_s.at[off], w_r.at[d], (dp_peer(off), s)) for off in range(1, n_dp)]
-    w_in = [remote(wup_ref.at[dp_peer(off)], upg.at[dp_peer(off)], w_s.at[off], w_r.at[dp_peer(off)], (sibling, s)) for off in range(1, n_dp)]
+    w_out = [remote(wout.at[dp_peer(off)], upg.at[d], w_s.at[off], w_r.at[d], (dp_peer(off), s)) for off in range(1, n_dp)]
+    w_in = [remote(wout.at[dp_peer(off)], upg.at[dp_peer(off)], w_s.at[off], w_r.at[dp_peer(off)], (sibling, s)) for off in range(1, n_dp)]
     for copy in w_out:
         copy.start()
     for copy in dm_first:
         copy.start()
-    upg[d] = wup_ref[d]
-
-    wide = xpad.shape[1]
-    for padded in (xpad, gpad):
-        padded[...] = jnp.zeros(padded.shape, F32)
-    xpad[margin:margin + rows, EDGE:EDGE + cols] = x_ref[...].astype(F32)
+
     halo_land(hx, halo_x, xpad)
 
     def convolve(padded, flip, lanes):
@@ -142,9 +147,9 @@
             first = EDGE - margin + b
             window = padded[:, first:first + cols, lanes]
             for a in range(taps):
-                tap = a * taps + b
-                tap = taps * taps - 1 - tap if flip else tap
-                total = total + kern_ref[tap:tap + 1, lanes].reshape(1, 1, LANES) * window[a:a + rows]
+                at = (taps - 1 - a, taps - 1 - b) if flip else (a, b)
+                tap = kern_ref[at[0], at[1]:at[1] + 1, lanes].reshape(1, 1, LANES)
+                total = total + tap * window[a:a + rows]
         return total
 
     def lanes_of(c):
@@ -201,7 +206,9 @@
         grad = (nt(dmx[slot], wdown_ref[...]) * slope).astype(BF16)
         hid[slot] = act
         dpre[slot] = grad
-        return nt(grad, up), nn(act, wdown_ref[...])
+        mixed = nn(act, wdown_ref[...])
+        dscale[...] += jnp.sum(dmx[slot].astype(F32) * mixed, axis=0, keepdims=True)
+        return nt(grad, up), mixed
 
     @pl.loop(0, chips)
     def _(i):
@@ -221,7 +228,6 @@
         home_copy(home_n, to).start()
         cross(cross_m, to).wait_recv()
         chip_m[to] = (mixed + r1m[to].astype(F32)).astype(BF16)
-        home_copy(home_m, to).start()
 
     normed, mixed = products(d)
     cross(cross_n, chip).wait_recv()
@@ -229,17 +235,26 @@
     cross(cross_m, chip).wait_recv()
     own_m[...] = mixed + r1m[chip].astype(F32)
 
-    strip = width // n_sp
-    part_rows = strip // share
+    part_rows = gsend.shape[2]
     flat = (n_dp * pixels,)
     for which, (left, right) in enumerate(((tok, dpre), (dmx, hid))):
-        gpart[which] = tn(left[...].reshape(flat + (width,)), right[...].reshape(flat + (hidden,)))
-        for k in range(n_sp):
-            gsend[k, which] = gpart[which, k * strip:(k + 1) * strip].astype(BF16)
-    gz_out = [remote(gsend.at[sp_peer(off)], grecv.at[s], gz_s.at[off], gz_r.at[s], (d, sp_peer(off))) for off in range(1, n_sp)]
-    gz_in = [remote(gsend.at[sp_peer(off)], grecv.at[sp_peer(off)], gz_s.at[off], gz_r.at[sp_peer(off)], (d, sp_peer(off))) for off in range(1, n_sp)]
-    for copy in gz_out:
-        copy.start()
+        summed = tn(left[...].reshape(flat + (width,)), right[...].reshape(flat + (hidden,)))
+        for t in range(n_dp):
+            gsend[t, which] = summed[t * part_rows:(t + 1) * part_rows].astype(BF16)
+    slot_out = place * n_sp + s
+    own_home = home == s
+
+    def owner_copy(off):
+        to = dp_peer(off)
+        return remote(gsend.at[to], grecv.at[slot_out], gz_s.at[off], gz_r.at[slot_out], (to, home))
+
+    for off in range(1, n_dp):
+        owner_copy(off).start()
+    pl.when(jnp.logical_not(own_home))(owner_copy(0).start)
+
+    @pl.when(own_home)
+    def _():
+        grecv[slot_out] = gsend[d]
 
     def arrive(got, send, recv, own):
         total = own[...]
@@ -250,6 +265,8 @@
         return total
 
     d_norm = arrive(r2n, bn_s, bn_r, own_n)
+    for off in range(1, chips):
+        home_copy(home_m, lax.rem(chip + off, chips)).start()
     normal = scaled_ref[...]
     d_hat = d_norm * gain_ref[...]
     lead = jnp.mean(d_hat, axis=-1, keepdims=True)
@@ -265,10 +282,10 @@
     def put(row, lanes, value):
         small[row // per, row % per:row % per + 1, lanes] = value
 
-    small[...] = jnp.zeros(small.shape, F32)
     everything = slice(None)
     put(count, everything, jnp.sum(d_norm * normal, axis=0, keepdims=True))
     put(count + 1, everything, jnp.sum(d_norm, axis=0, keepdims=True))
+    put(count + 2, everything, dscale[...] / scale_ref[...])
 
     @pl.loop(0, width // LANES)
     def _(c):
@@ -281,33 +298,19 @@
                 product = jnp.sum(window[a:a + rows] * upstream, axis=0)
                 put(a * taps + b, lanes, jnp.sum(product, axis=0, keepdims=True))
 
-    mixed = arrive(r2m, bm_s, bm_r, own_m)
-    res_ref[...] = (x_ref[...].reshape(pixels, width).astype(F32) + scale_ref[...] * mixed).astype(BF16).reshape(rows, cols, width)
-    put(count + 2, everything, jnp.sum(cot_ref[...].astype(F32) * mixed, axis=0, keepdims=True))
-
     s1_out = [remote(small.at[dp_peer(off)], ar1.at[d], s1_s.at[off], s1_r.at[d], (dp_peer(off), s)) for off in range(1, n_dp)]
     s1_in = [remote(small.at[dp_peer(off)], ar1.at[dp_peer(off)], s1_s.at[off], s1_r.at[dp_peer(off)], (sibling, s)) for off in range(1, n_dp)]
     for copy in s1_out:
         copy.start()
     ar1[d] = small[d]
 
-    for copy in gz_in:
-        copy.wait_recv()
-    for which in range(2):
-        total = gpart[which, pl.ds(pl.multiple_of(s * strip, strip), strip)]
-        for off in range(1, n_sp):
-            total = total + grecv[sp_peer(off), which].astype(F32)
-        for b in range(share):
-            fsend[b, which] = total[b * part_rows:(b + 1) * part_rows].astype(BF16)
-    for b in range(share):
-        own_block = jnp.logical_and(home == s, place == b)
-        copy = remote(fsend.at[b], frecv.at[place], fi_s.at[b], fi_r.at[place], (s * share + b, home))
-
-        pl.when(jnp.logical_not(own_block))(copy.start)
-
-        @pl.when(own_block)
-        def _():
-            frecv[b] = fsend[b]
+    halo_land(hg, halo_g, gpad)
+
+    @pl.loop(0, width // LANES)
+    def _(c):
+        lanes = lanes_of(c)
+        cot = cot_ref[:, lanes].astype(F32).reshape(rows, cols, LANES)
+        dfeat_ref[:, :, lanes] = cot + convolve(gpad, True, lanes)
 
     for copy in s1_in:
         copy.wait_recv()
@@ -317,13 +320,8 @@
     for copy in s2_out:
         copy.start()
 
-    halo_land(hg, halo_g, gpad)
-
-    @pl.loop(0, width // LANES)
-    def _(c):
-        lanes = lanes_of(c)
-        cot = cot_ref[:, lanes].astype(F32).reshape(rows, cols, LANES)
-        dfeat_ref[:, :, lanes] = cot + convolve(gpad, True, lanes)
+    mixed = arrive(r2m, bm_s, bm_r, own_m)
+    res_ref[...] = (x_ref[...].reshape(pixels, width).astype(F32) + scale_ref[...] * mixed).astype(BF16).reshape(rows, cols, width)
 
     for copy in s2_in:
         copy.wait_recv()
@@ -333,27 +331,39 @@
     for copy in s3_out:
         copy.start()
 
-    for b in range(share):
-        own_block = jnp.logical_and(home == s, place == b)
-        copy = remote(fsend.at[b], frecv.at[b], fi_s.at[b], fi_r.at[b], (s * share + b, home))
-        pl.when(jnp.logical_not(own_block))(copy.wait_recv)
-    for b in range(share):
-        gup_ref[:, b * hidden:(b + 1) * hidden] = frecv[b, 0].astype(F32)
-        gdown_ref[:, b * hidden:(b + 1) * hidden] = frecv[b, 1].astype(F32)
+    for j in range(share):
+        sums = [None, None]
+        for k in range(n_sp):
+            slot = j * n_sp + k
+            landed = remote(gsend.at[0], grecv.at[slot], gz_s.at[0], gz_r.at[slot], (sibling, s))
+            pl.when(jnp.logical_not(is_self(j, k)))(landed.wait_recv)
+            for which in range(2):
+                part = grecv[slot, which].astype(F32)
+                sums[which] = part if k == 0 else sums[which] + part
+        gup_ref[:, j * hidden:(j + 1) * hidden] = sums[0]
+        gdown_ref[:, j * hidden:(j + 1) * hidden] = sums[1]
 
     for copy in s3_in:
         copy.wait_recv()
-    small_ref[...] = ar3[...]
+
+    def take(row):
+        return ar3[row // per, row % per:row % per + 1]
+
+    for a in range(taps):
+        for b in range(taps):
+            gkern_ref[a, b:b + 1] = take(a * taps + b)
+    ggain_ref[...] = take(count)
+    gbias_ref[...] = take(count + 1)
+    gscale_ref[...] = take(count + 2)
 
     halo_sent(hx)
     halo_sent(hg)
-    for group in (w_out, dm_first, dm_passed, tk_first, tk_passed, gz_out, s1_out, s2_out, s3_out):
+    for group in (w_out, dm_first, dm_passed, tk_first, tk_passed, s1_out, s2_out, s3_out):
         for copy in group:
             copy.wait_send()
-    for b in range(share):
-        own_block = jnp.logical_and(home == s, place == b)
-        copy = remote(fsend.at[b], frecv.at[b], fi_s.at[b], fi_r.at[b], (s * share + b, home))
-        pl.when(jnp.logical_not(own_block))(copy.wait_send)
+    for off in range(1, n_dp):
+        owner_copy(off).wait_send()
+    pl.when(jnp.logical_not(own_home))(owner_copy(0).wait_send)
 
     for off in range(chips):
         to = lax.rem(chip + 1 + off, chips)
@@ -372,11 +382,10 @@
     pixels = rows * cols
     hidden = w_down.shape[0]
     chips, share = n_dp // 2, n_dp // n_sp
-    strip = width // n_sp
-    part_rows = strip // share
+    part_rows = width // n_dp
     count = taps * taps
     per = -(-(count + 3) // n_dp)
-    outgoing = w_up.reshape(w_up.shape[0], n_dp, hidden).transpose(1, 0, 2)
+    blocks = (n_dp, w_up.shape[0], hidden)
     padded = (rows + 2 * margin, cols + 2 * EDGE, width)
     dma = lambda k: pltpu.SemaphoreType.DMA((k,))
     vm = pltpu.VMEM
@@ -384,33 +393,33 @@
         vm(padded, F32), vm(padded, F32),
         vm((2, margin, cols, width), BF16), vm((2, margin, cols, width), BF16),
         vm((pixels, width), F32), vm((pixels, width), F32), vm((rows, cols, width), BF16),
-        vm(outgoing.shape, BF16),
+        vm(blocks, BF16), vm(blocks, BF16),
         vm((n_dp, pixels, width), BF16), vm((n_dp, pixels, width), BF16),
         vm((n_dp, pixels, hidden), BF16), vm((n_dp, pixels, hidden), BF16),
     ]
     scratch += [vm((chips, pixels, width), BF16)] * 8
     scratch += [vm((pixels, width), F32)] * 2
     scratch += [
-        vm((2, width, hidden), F32),
-        vm((n_sp, 2, strip, hidden), BF16), vm((n_sp, 2, strip, hidden), BF16),
-        vm((share, 2, part_rows, hidden), BF16), vm((share, 2, part_rows, hidden), BF16),
+        vm((n_dp, 2, part_rows, hidden), BF16), vm((n_dp, 2, part_rows, hidden), BF16),
+        vm((1, width), F32),
         vm((n_dp, per, width), F32), vm((n_dp, per, width), F32),
         vm((n_sp, per, width), F32), vm((n_dp, per, width), F32),
     ]
     scratch += [dma(2)] * 4 + [dma(n_dp)] * 6 + [dma(chips)] * 8
-    scratch += [dma(n_sp)] * 2 + [dma(share)] * 2 + [dma(n_dp)] * 2 + [dma(n_sp)] * 2 + [dma(n_dp)] * 2
+    scratch += [dma(n_dp)] * 4 + [dma(n_sp)] * 2 + [dma(n_dp)] * 2
     whole = pl.BlockSpec(memory_space=pltpu.VMEM)
-    result, d_feat, grad_up, grad_down, small = pl.pallas_call(
+    result, d_feat, grad_up, grad_down, kernel_sum, gain_sum, bias_sum, scale_sum = pl.pallas_call(
         functools.partial(block_kernel, (n_dp, n_sp, rows, cols, width, taps)),
         out_shape=(
             jax.ShapeDtypeStruct((rows, cols, width), BF16),
             jax.ShapeDtypeStruct((rows, cols, width), F32),
             jax.ShapeDtypeStruct((part_rows, share * hidden), F32),
             jax.ShapeDtypeStruct((part_rows, share * hidden), F32),
-            jax.ShapeDtypeStruct((n_dp, per, width), F32),
-        ),
+            jax.ShapeDtypeStruct((taps, taps, width), F32),
+        )
+        + (jax.ShapeDtypeStruct((1, width), F32),) * 3,
         in_specs=[whole] * 8,
-        out_specs=(whole,) * 5,
+        out_specs=(whole,) * 8,
         scratch_shapes=scratch,
         compiler_params=pltpu.CompilerParams(
             collective_id=0, has_side_effects=True, vmem_limit_bytes=60 << 20
@@ -418,24 +427,23 @@
     )(
         features[0],
         cotangent[0].reshape(pixels, width),
-        dw_kernel.reshape(count, width),
+        dw_kernel,
         ln_gain.reshape(1, width),
         ln_bias.reshape(1, width),
         layer_scale.reshape(1, width),
-        outgoing,
+        w_up,
         w_down,
     )
     regions = float(n_dp)
-    small = small.reshape(n_dp * per, width) / regions
     return (
         result[None],
         d_feat[None],
         grad_up / regions,
         grad_down.T / regions,
-        small[:count].reshape(taps, taps, width),
-        small[count],
-        small[count + 1],
-        small[count + 2],
+        kernel_sum / regions,
+        gain_sum[0] / regions,
+        bias_sum[0] / regions,
+        scale_sum[0] / regions,
     )
 
 

time: 65.8 us -> 84.4 us (1.28)
  Pallas kernels: 57.1 us -> 77.7 us
  local copies, waits for them, and re-layouts: 6.17 us -> 2.33 us
  other arithmetic: 1.64 us -> 3.44 us
    pallas_call x1, Pallas kernels: 57.1 us -> 77.7 us  [local(): pl.pallas_call(functools.partial(block_kernel, (n_dp, n_sp, rows, cols, w...]
    reshape x2 -> x0, local copies, waits for them, and re-layouts: 3.23 us -> none  [the longest x1 1.67 us: local(): outgoing = w_up.reshape(w_up.shape[0], n_dp, hidden).transpose(1, 0, 2)]
    div x1 -> x3, other arithmetic: 0.92 us -> 2.72 us  [the longest x1 1.55 us: local(): kernel_sum / regions]
    slice x2 -> x0, local copies, waits for them, and re-layouts: 1.24 us -> none  [the longest x1 0.65 us: local(): small[:count].reshape(taps, taps, width)]
    unnamed x10 -> x16, local copies, waits for them, and re-layouts: 1.68 us -> 2.33 us
where the time goes in v2:
time: 84.4 us; the launch traced here: 84.2 us
  Pallas kernels  77.7 us (92%)
  other arithmetic  3.44 us (4%)
  local copies, waits for them, and re-layouts  2.33 us (3%)
    pallas_call x1, Pallas kernels, local(): pl.pallas_call(functools.partial(block_kernel, (n_dp, n_sp, rows, cols, w...  77.7 us
    unnamed x16, local copies, waits for them, and re-layouts  2.33 us

profile of v2, /device:TPU:0, one launch (start us, length us, event | category | flops | bytes accessed | tf_op | source)
XLA Modules:
  0.0 84.2 jit_solution(1133518953089244862)
XLA Ops:
  0.6 77.7 %shard_map.143 = (bf16[8,16,512]{2,1,0:T(8,128)(2,1)}, f32[8,16,512]{2,1,0:T(8,128)}, f32[64,512]{1,0:T(8,128)}, f32[64,512]{1,0:T(8,128)}, f32[7,7,512]{2,1,0:T...) custom-call(bf16[8,16,512]{2,1,0:T(8,128)(2,1)} %bitcast.13, bf16[128,512]{1,0:T(8,128)(2,1)} %bitcast.14, ...), custom_call_target="tpu_custom_call" | custom-call | tf_op jit(solution)/shard_map/pallas_call | solution.py:411
  78.4 0.0 copy-start.6
  78.4 0.0 copy-start.5
  78.4 0.0 copy-start.4
  78.4 0.0 copy-start.2
  78.4 0.0 copy-start.3
  78.4 0.6 copy-done.4
  79.1 0.6 broadcast_multiply_fusion.4
  79.7 0.0 copy-done.6
  79.7 0.0 copy-done.5
  79.7 0.6 broadcast_multiply_fusion.2
  80.3 1.6 %broadcast_multiply_fusion.1 = f32[7,7,512]{2,1,0:T(8,128)} fusion(f32[7,7,512]{2,1,0:T(8,128)} %get-tuple-element.20), kind=kLoop, calls=%fused_computation.2 | loop fusion | flops 25088 | bytes 200704 | tf_op jit(solution)/shard_map/div | solution.py:443
  81.8 0.0 copy-done.2
  81.8 0.0 copy-done.3
  81.8 0.0 copy-start.1
  81.8 0.7 multiply_bitcast_fusion
  82.5 0.0 copy-start
  82.5 0.2 copy-done.1
  82.8 0.7 copy.18
  83.4 0.1 copy-done
  83.5 0.7 copy.19
Async XLA Ops:
  78.4 1.3 %copy-start.6 = (f32[1,512]{1,0:T(1,128)S(1)}, f32[1,512]{1,0:T(1,128)}, u32[]{:S(2)}) copy-start(f32[1,512]{1,0:T(1,128)} %get-tuple-element.23) | copy-start | bytes 6148
  78.4 1.3 %copy-start.5 = (f32[1,512]{1,0:T(1,128)S(1)}, f32[1,512]{1,0:T(1,128)}, u32[]{:S(2)}) copy-start(f32[1,512]{1,0:T(1,128)} %get-tuple-element.22) | copy-start | bytes 6148
  78.4 0.7 copy-start.4
  78.4 3.4 %copy-start.2 = (f32[64,512]{1,0:T(8,128)S(1)}, f32[64,512]{1,0:T(8,128)}, u32[]{:S(2)}) copy-start(f32[64,512]{1,0:T(8,128)} %get-tuple-element.18) | copy-start | bytes 393220
  78.4 3.4 %copy-start.3 = (f32[64,512]{1,0:T(8,128)S(1)}, f32[64,512]{1,0:T(8,128)}, u32[]{:S(2)}) copy-start(f32[64,512]{1,0:T(8,128)} %get-tuple-element.19) | copy-start | bytes 393220
  81.8 1.0 %copy-start.1 = (bf16[8,16,512]{2,1,0:T(8,128)(2,1)S(1)}, bf16[8,16,512]{2,1,0:T(8,128)(2,1)}, u32[]{:S(2)}) copy-start(bf16[8,16,512]{2,1,0:T(8,128)(2,1)} %get-tuple-element.16) | copy-start | bytes 393220
  82.5 1.0 %copy-start = (f32[8,16,512]{2,1,0:T(8,128)S(1)}, f32[8,16,512]{2,1,0:T(8,128)}, u32[]{:S(2)}) copy-start(f32[8,16,512]{2,1,0:T(8,128)} %get-tuple-element.17) | copy-start | bytes 786436

commit v3 on v2

--- a/solution.py
+++ b/solution.py
@@ -36,10 +36,10 @@
     res_ref, dfeat_ref, gup_ref, gdown_ref, gkern_ref, ggain_ref, gbias_ref, gscale_ref,
     xpad, gpad, halo_x, halo_g, conv, scaled_ref, dconv, wout, upg, tok, dmx, hid, dpre,
     part_n, part_m, r1n, r1m, chip_n, chip_m, r2n, r2m, own_n, own_m,
-    gsend, grecv, dscale, small, ar1, ar2, ar3,
+    gpart, gsend, grecv, fsend, frecv, dscale, small, ar1, ar2, ar3,
     hx_s, hx_r, hg_s, hg_r, w_s, w_r, dm_s, dm_r, tk_s, tk_r,
     an_s, an_r, am_s, am_r, bn_s, bn_r, bm_s, bm_r,
-    gz_s, gz_r, s1_s, s1_r, s2_s, s2_r, s3_s, s3_r,
+    gz_s, gz_r, fi_s, fi_r, s1_s, s1_r, s2_s, s2_r, s3_s, s3_r,
 ):
     n_dp, n_sp, rows, cols, width, taps = sizes
     chips, share = n_dp // 2, n_dp // n_sp
@@ -53,8 +53,8 @@
     place = lax.rem(d, share)
     inside = (home == s).astype(jnp.int32)
 
-    def is_self(j, k):
-        return jnp.logical_and(jnp.logical_and(home == s, place == j), s == k)
+    def is_self(b):
+        return jnp.logical_and(home == s, place == b)
 
     def dp_peer(off):
         return lax.rem(d + off, n_dp)
@@ -71,11 +71,10 @@
         greet((dp_peer(off), s))
     for off in range(1, n_sp):
         greet((d, sp_peer(off)))
-    for j in range(share):
-        for k in range(n_sp):
-            @pl.when(jnp.logical_not(is_self(j, k)))
-            def _():
-                greet((s * share + j, jnp.int32(k)))
+    for b in range(share):
+        @pl.when(jnp.logical_not(is_self(b)))
+        def _():
+            greet((s * share + b, home))
 
     dmx[d] = (scale_ref[...] * cot_ref[...].astype(F32)).astype(BF16)
     for t in range(n_dp):
@@ -86,7 +85,7 @@
     xpad[margin:margin + rows, EDGE:EDGE + cols] = x_ref[...].astype(F32)
     dscale[...] = jnp.zeros(dscale.shape, F32)
     small[...] = jnp.zeros(small.shape, F32)
-    pl.semaphore_wait(barrier, (n_dp - 1) + (n_sp - 1) + n_dp - inside)
+    pl.semaphore_wait(barrier, (n_dp - 1) + (n_sp - 1) + share - inside)
 
     has_up, has_down = s > 0, s < n_sp - 1
 
@@ -235,26 +234,21 @@
     cross(cross_m, chip).wait_recv()
     own_m[...] = mixed + r1m[chip].astype(F32)
 
-    part_rows = gsend.shape[2]
+    strip = width // n_sp
+    part_rows = strip // share
     flat = (n_dp * pixels,)
+
+    def plane_copy(which, off, landing):
+        to = sp_peer(off)
+        slot = to if landing else s
+        return remote(gsend.at[which, to], grecv.at[which, slot], gz_s.at[which, off], gz_r.at[which, slot], (d, to))
+
     for which, (left, right) in enumerate(((tok, dpre), (dmx, hid))):
-        summed = tn(left[...].reshape(flat + (width,)), right[...].reshape(flat + (hidden,)))
-        for t in range(n_dp):
-            gsend[t, which] = summed[t * part_rows:(t + 1) * part_rows].astype(BF16)
-    slot_out = place * n_sp + s
-    own_home = home == s
-
-    def owner_copy(off):
-        to = dp_peer(off)
-        return remote(gsend.at[to], grecv.at[slot_out], gz_s.at[off], gz_r.at[slot_out], (to, home))
-
-    for off in range(1, n_dp):
-        owner_copy(off).start()
-    pl.when(jnp.logical_not(own_home))(owner_copy(0).start)
-
-    @pl.when(own_home)
-    def _():
-        grecv[slot_out] = gsend[d]
+        gpart[which] = tn(left[...].reshape(flat + (width,)), right[...].reshape(flat + (hidden,)))
+        for k in range(n_sp):
+            gsend[which, k] = gpart[which, k * strip:(k + 1) * strip].astype(BF16)
+        for off in range(1, n_sp):
+            plane_copy(which, off, False).start()
 
     def arrive(got, send, recv, own):
         total = own[...]
@@ -320,6 +314,22 @@
     for copy in s2_out:
         copy.start()
 
+    def owner_copy(which, b):
+        return remote(fsend.at[which, b], frecv.at[which, place], fi_s.at[which, b], fi_r.at[which, place], (s * share + b, home))
+
+    for which in range(2):
+        total = gpart[which, pl.ds(pl.multiple_of(s * strip, strip), strip)]
+        for off in range(1, n_sp):
+            plane_copy(which, off, True).wait_recv()
+            total = total + grecv[which, sp_peer(off)].astype(F32)
+        for b in range(share):
+            fsend[which, b] = total[b * part_rows:(b + 1) * part_rows].astype(BF16)
+            pl.when(jnp.logical_not(is_self(b)))(owner_copy(which, b).start)
+
+            @pl.when(is_self(b))
+            def _():
+                frecv[which, b] = fsend[which, b]
+
     mixed = arrive(r2m, bm_s, bm_r, own_m)
     res_ref[...] = (x_ref[...].reshape(pixels, width).astype(F32) + scale_ref[...] * mixed).astype(BF16).reshape(rows, cols, width)
 
@@ -331,17 +341,12 @@
     for copy in s3_out:
         copy.start()
 
-    for j in range(share):
-        sums = [None, None]
-        for k in range(n_sp):
-            slot = j * n_sp + k
-            landed = remote(gsend.at[0], grecv.at[slot], gz_s.at[0], gz_r.at[slot], (sibling, s))
-            pl.when(jnp.logical_not(is_self(j, k)))(landed.wait_recv)
-            for which in range(2):
-                part = grecv[slot, which].astype(F32)
-                sums[which] = part if k == 0 else sums[which] + part
-        gup_ref[:, j * hidden:(j + 1) * hidden] = sums[0]
-        gdown_ref[:, j * hidden:(j + 1) * hidden] = sums[1]
+    for which, out in enumerate((gup_ref, gdown_ref)):
+        for b in range(share):
+            landed = remote(fsend.at[which, b], frecv.at[which, b], fi_s.at[which, b], fi_r.at[which, b], (sibling, s))
+            pl.when(jnp.logical_not(is_self(b)))(landed.wait_recv)
+        for b in range(share):
+            out[:, b * hidden:(b + 1) * hidden] = frecv[which, b].astype(F32)
 
     for copy in s3_in:
         copy.wait_recv()
@@ -361,9 +366,11 @@
     for group in (w_out, dm_first, dm_passed, tk_first, tk_passed, s1_out, s2_out, s3_out):
         for copy in group:
             copy.wait_send()
-    for off in range(1, n_dp):
-        owner_copy(off).wait_send()
-    pl.when(jnp.logical_not(own_home))(owner_copy(0).wait_send)
+    for which in range(2):
+        for off in range(1, n_sp):
+            plane_copy(which, off, False).wait_send()
+        for b in range(share):
+            pl.when(jnp.logical_not(is_self(b)))(owner_copy(which, b).wait_send)
 
     for off in range(chips):
         to = lax.rem(chip + 1 + off, chips)
@@ -382,7 +389,8 @@
     pixels = rows * cols
     hidden = w_down.shape[0]
     chips, share = n_dp // 2, n_dp // n_sp
-    part_rows = width // n_dp
+    strip = width // n_sp
+    part_rows = strip // share
     count = taps * taps
     per = -(-(count + 3) // n_dp)
     blocks = (n_dp, w_up.shape[0], hidden)
@@ -400,13 +408,16 @@
     scratch += [vm((chips, pixels, width), BF16)] * 8
     scratch += [vm((pixels, width), F32)] * 2
     scratch += [
-        vm((n_dp, 2, part_rows, hidden), BF16), vm((n_dp, 2, part_rows, hidden), BF16),
+        vm((2, width, hidden), F32),
+        vm((2, n_sp, strip, hidden), BF16), vm((2, n_sp, strip, hidden), BF16),
+        vm((2, share, part_rows, hidden), BF16), vm((2, share, part_rows, hidden), BF16),
         vm((1, width), F32),
         vm((n_dp, per, width), F32), vm((n_dp, per, width), F32),
         vm((n_sp, per, width), F32), vm((n_dp, per, width), F32),
     ]
     scratch += [dma(2)] * 4 + [dma(n_dp)] * 6 + [dma(chips)] * 8
-    scratch += [dma(n_dp)] * 4 + [dma(n_sp)] * 2 + [dma(n_dp)] * 2
+    pair = lambda k: pltpu.SemaphoreType.DMA((2, k))
+    scratch += [pair(n_sp)] * 2 + [pair(share)] * 2 + [dma(n_dp)] * 2 + [dma(n_sp)] * 2 + [dma(n_dp)] * 2
     whole = pl.BlockSpec(memory_space=pltpu.VMEM)
     result, d_feat, grad_up, grad_down, kernel_sum, gain_sum, bias_sum, scale_sum = pl.pallas_call(
         functools.partial(block_kernel, (n_dp, n_sp, rows, cols, width, taps)),

time: 84.4 us -> 63.8 us (0.76)
  Pallas kernels: 77.7 us -> 56.5 us
    pallas_call x1, Pallas kernels: 77.7 us -> 56.5 us  [local(): pl.pallas_call(functools.partial(block_kernel, (n_dp, n_sp, rows, cols, w...]
where the time goes in v3:
time: 63.8 us; the launch traced here: 62.9 us
  Pallas kernels  56.5 us (89%)
  other arithmetic  3.44 us (5%)
  local copies, waits for them, and re-layouts  2.33 us (4%)
  between operations  0.69 us (1%)
    pallas_call x1, Pallas kernels, local(): pl.pallas_call(functools.partial(block_kernel, (n_dp, n_sp, rows, cols, w...  56.5 us
    unnamed x16, local copies, waits for them, and re-layouts  2.33 us
    div x1, other arithmetic, local(): kernel_sum / regions  1.55 us

profile of v3, /device:TPU:0, one launch (start us, length us, event | category | flops | bytes accessed | tf_op | source)
XLA Modules:
  0.0 62.9 jit_solution(5788348516922951866)
XLA Ops:
  0.6 56.5 %shard_map.143 = (bf16[8,16,512]{2,1,0:T(8,128)(2,1)}, f32[8,16,512]{2,1,0:T(8,128)}, f32[64,512]{1,0:T(8,128)}, f32[64,512]{1,0:T(8,128)}, f32[7,7,512]{2,1,0:T...) custom-call(bf16[8,16,512]{2,1,0:T(8,128)(2,1)} %bitcast.13, bf16[128,512]{1,0:T(8,128)(2,1)} %bitcast.14, ...), custom_call_target="tpu_custom_call" | custom-call | tf_op jit(solution)/shard_map/pallas_call | solution.py:422
  57.1 0.0 copy-start.6
  57.1 0.0 copy-start.5
  57.1 0.0 copy-start.4
  57.2 0.0 copy-start.2
  57.2 0.0 copy-start.3
  57.2 0.6 %copy-done.4 = f32[1,512]{1,0:T(1,128)S(1)} copy-done((f32[1,512]{1,0:T(1,128)S(1)}, f32[1,512]{1,0:T(1,128)}, u32[]{:S(2)}) %copy-start.4) | copy-done | bytes 2072
  57.8 0.6 broadcast_multiply_fusion.4
  58.4 0.0 copy-done.6
  58.4 0.0 copy-done.5
  58.4 0.6 broadcast_multiply_fusion.2
  59.0 1.6 %broadcast_multiply_fusion.1 = f32[7,7,512]{2,1,0:T(8,128)} fusion(f32[7,7,512]{2,1,0:T(8,128)} %get-tuple-element.20), kind=kLoop, calls=%fused_computation.2 | loop fusion | flops 25088 | bytes 200704 | tf_op jit(solution)/shard_map/div | solution.py:454
  60.5 0.0 copy-done.2
  60.6 0.0 copy-done.3
  60.6 0.0 copy-start.1
  60.6 0.7 %multiply_bitcast_fusion = (f32[512,64]{0,1:T(8,128)}, f32[64,512]{1,0:T(8,128)}) fusion(f32[64,512]{1,0:T(8,128)S(1)} %copy-done.3, f32[64,512]{1,0:T(8,128)S(1)} %copy-done.2), kind=kLoop, calls=%fused_computation | loop fusion | flops 65536 | bytes 524288 | tf_op jit(solution)/shard_map/div | solution.py:453
  61.3 0.0 copy-start
  61.3 0.2 copy-done.1
  61.5 0.7 %copy.18 = bf16[1,8,16,512]{3,2,1,0:T(8,128)(2,1)} copy(bf16[1,8,16,512]{3,2,1,0:T(8,128)(2,1)S(1)} %bitcast.15) | data formatting | bytes 262144
  62.2 0.1 copy-done
  62.2 0.7 %copy.19 = f32[1,8,16,512]{3,2,1,0:T(8,128)} copy(f32[1,8,16,512]{3,2,1,0:T(8,128)S(1)} %bitcast.12) | data formatting | bytes 524288
Async XLA Ops:
  57.1 1.3 %copy-start.6 = (f32[1,512]{1,0:T(1,128)S(1)}, f32[1,512]{1,0:T(1,128)}, u32[]{:S(2)}) copy-start(f32[1,512]{1,0:T(1,128)} %get-tuple-element.23) | copy-start | bytes 6148
  57.1 1.3 %copy-start.5 = (f32[1,512]{1,0:T(1,128)S(1)}, f32[1,512]{1,0:T(1,128)}, u32[]{:S(2)}) copy-start(f32[1,512]{1,0:T(1,128)} %get-tuple-element.22) | copy-start | bytes 6148
  57.1 0.7 %copy-start.4 = (f32[1,512]{1,0:T(1,128)S(1)}, f32[1,512]{1,0:T(1,128)}, u32[]{:S(2)}) copy-start(f32[1,512]{1,0:T(1,128)} %get-tuple-element.21) | copy-start | bytes 6148
  57.2 3.4 %copy-start.2 = (f32[64,512]{1,0:T(8,128)S(1)}, f32[64,512]{1,0:T(8,128)}, u32[]{:S(2)}) copy-start(f32[64,512]{1,0:T(8,128)} %get-tuple-element.18) | copy-start | bytes 393220
  57.2 3.4 %copy-start.3 = (f32[64,512]{1,0:T(8,128)S(1)}, f32[64,512]{1,0:T(8,128)}, u32[]{:S(2)}) copy-start(f32[64,512]{1,0:T(8,128)} %get-tuple-element.19) | copy-start | bytes 393220
  60.6 1.0 %copy-start.1 = (bf16[8,16,512]{2,1,0:T(8,128)(2,1)S(1)}, bf16[8,16,512]{2,1,0:T(8,128)(2,1)}, u32[]{:S(2)}) copy-start(bf16[8,16,512]{2,1,0:T(8,128)(2,1)} %get-tuple-element.16) | copy-start | bytes 393220
  61.3 1.0 %copy-start = (f32[8,16,512]{2,1,0:T(8,128)S(1)}, f32[8,16,512]{2,1,0:T(8,128)}, u32[]{:S(2)}) copy-start(f32[8,16,512]{2,1,0:T(8,128)} %get-tuple-element.17) | copy-start | bytes 786436
